TPU v7x, 512 devices: a whole 4x4x16 slice. The times are simulated.
512 devices in a mesh: gx: 128 (over y, z, core), gy: 4 (over x).
Axes of the slice: x: 4, y: 4, z: 16, core: 2. Of those that a mesh axis runs over, the one named last changes fastest.
Arguments:
- populations: float32 [256, 19, 64, 256], P('gx', None, 'gy'), may hold values from 0.013 to 0.5, as said below
- cotangent: bfloat16 [256, 19, 64, 256], P('gx', None, 'gy'), may hold values from -12 to 12
- flags: int32 [256, 64, 256], P('gx', 'gy'), may hold values 0 or 1
- w_in: bfloat16 [128, 19], replicated, may hold values from -4 to 4
- b_in: float32 [128], replicated, may hold values from -3 to 3
- w_out: bfloat16 [19, 128], replicated, may hold values from -0.02734375 to 0.02734375
Outputs:
- adjoint_pops: bfloat16 [256, 19, 64, 256], P('gx', None, 'gy')
- grad_w_in: float32 [128, 19], replicated
- grad_b_in: float32 [128], replicated
- grad_w_out: float32 [19, 128], replicated
Inputs may be any that keep to these rules, and one draw needn't show every extreme that they name: populations are positive at every cell and velocity.
All inputs are finite; a program needn't handle non-finite values. No bound on the sum of `flags` on one device may be relied on, other than what follows from the above.
Results may differ from a plain program's by a relative error of at most 0.012.
The roundings to bfloat16 on the way count: a program that leaves them out, or rounds other values in their place, can miss the bound.
Values sent between devices are 32-bit elements; how exact they have to be, the bound alone decides.
A program may use at most 64 MiB of HBM per device.

v0:
```python
import jax
import jax.numpy as jnp
from jax import lax
from jax.sharding import PartitionSpec as P

VELOCITY = [
    (0, 0, 0),
    (1, 0, 0),
    (-1, 0, 0),
    (0, 1, 0),
    (0, -1, 0),
    (0, 0, 1),
    (0, 0, -1),
    (1, 1, 0),
    (-1, -1, 0),
    (1, -1, 0),
    (-1, 1, 0),
    (1, 0, 1),
    (-1, 0, -1),
    (1, 0, -1),
    (-1, 0, 1),
    (0, 1, 1),
    (0, -1, -1),
    (0, 1, -1),
    (0, -1, 1),
]
OPPOSITE = [0, 2, 1, 4, 3, 6, 5, 8, 7, 10, 9, 12, 11, 14, 13, 16, 15, 18, 17]
LATTICE_WEIGHTS = [1.0 / 3.0] + [1.0 / 18.0] * 6 + [1.0 / 36.0] * 12
TAU_INV = 1.25
BUOYANCY = 0.05


def padded_2(cells, sides, width):
    for axis, dim in sides:
        count = lax.axis_size(axis)
        head = lax.slice_in_dim(cells, 0, width, axis=dim)
        tail = lax.slice_in_dim(cells, cells.shape[dim] - width, cells.shape[dim], axis=dim)
        cells = jnp.concatenate(
            [
                lax.ppermute(tail, axis, [(i, (i + 1) % count) for i in range(count)]),
                cells,
                lax.ppermute(head, axis, [((i + 1) % count, i) for i in range(count)]),
            ],
            axis=dim,
        )
    return cells


def lattice_tables():
    vel_x = jnp.asarray([float(v[0]) for v in VELOCITY], jnp.float32)[:, None]
    vel_y = jnp.asarray([float(v[1]) for v in VELOCITY], jnp.float32)[:, None]
    vel_z = jnp.asarray([float(v[2]) for v in VELOCITY], jnp.float32)[:, None]
    weights = jnp.asarray(LATTICE_WEIGHTS, jnp.float32)[:, None]
    return (vel_x, vel_y, vel_z, weights)


def equilibrium_parts(pops):
    vel_x, vel_y, vel_z, weights = lattice_tables()
    density = jnp.sum(pops, axis=0)
    momentum_x = jnp.sum(vel_x * pops, axis=0)
    momentum_y = jnp.sum(vel_y * pops, axis=0)
    momentum_z = jnp.sum(vel_z * pops, axis=0)
    projected = vel_x * momentum_x + vel_y * momentum_y + vel_z * momentum_z
    momentum_sq = momentum_x * momentum_x + momentum_y * momentum_y + momentum_z * momentum_z
    equilibrium = weights * (
        density + 3.0 * projected + 4.5 * projected * projected - 1.5 * momentum_sq
    )
    return (density, (momentum_x, momentum_y, momentum_z), projected, equilibrium)


def network_front(pops, equilibrium, w_in, b_in):
    weights = lattice_tables()[3]
    features = ((pops - equilibrium) / weights).astype(jnp.bfloat16)
    preact = jnp.dot(w_in, features, preferred_element_type=jnp.float32) + b_in[:, None]
    return (features, preact)


def collide_plane(pops, melt, w_in, b_in, w_out):
    vel_x, vel_y, vel_z, weights = lattice_tables()
    density, momentum, projected, equilibrium = equilibrium_parts(pops)
    features, preact = network_front(pops, equilibrium, w_in, b_in)
    hidden = jnp.tanh(preact).astype(jnp.bfloat16)
    learned = jnp.dot(w_out, hidden, preferred_element_type=jnp.float32)
    lift = 3.0 * BUOYANCY * weights * vel_z
    relaxed = pops - TAU_INV * (pops - equilibrium) + learned + lift * (density - 1.0)
    bounced = jnp.stack([pops[k] for k in OPPOSITE], axis=0)
    return jnp.where(melt > 0.5, relaxed, bounced)


def adjoint_plane(pops, melt, incoming, w_in, b_in, w_out):
    vel_x, vel_y, vel_z, weights = lattice_tables()
    density, momentum, projected, equilibrium = equilibrium_parts(pops)
    features, preact = network_front(pops, equilibrium, w_in, b_in)
    activity = jnp.tanh(preact)
    hidden = activity.astype(jnp.bfloat16)
    melt_adj = incoming * melt
    solid_adj = incoming - melt_adj
    grad_out = melt_adj.astype(jnp.bfloat16)
    contract = (((1,), (1,)), ((), ()))
    grad_w_out = lax.dot_general(grad_out, hidden, contract, preferred_element_type=jnp.float32)
    grad_hidden = jnp.dot(w_out.T, grad_out, preferred_element_type=jnp.float32)
    grad_preact = (grad_hidden * (1.0 - activity * activity)).astype(jnp.bfloat16)
    grad_w_in = lax.dot_general(grad_preact, features, contract, preferred_element_type=jnp.float32)
    grad_b_in = jnp.sum(grad_preact, axis=1, dtype=jnp.float32)
    grad_noneq = jnp.dot(w_in.T, grad_preact, preferred_element_type=jnp.float32) / weights
    grad_equil = TAU_INV * melt_adj - grad_noneq
    weighted = weights * grad_equil
    lift = 3.0 * BUOYANCY * weights * vel_z
    grad_density = jnp.sum(weighted, axis=0) + jnp.sum(lift * melt_adj, axis=0)
    slope_terms = weighted * (3.0 + 9.0 * projected)
    weighted_total = jnp.sum(weighted, axis=0)
    grad_mx = jnp.sum(vel_x * slope_terms, axis=0) - 3.0 * momentum[0] * weighted_total
    grad_my = jnp.sum(vel_y * slope_terms, axis=0) - 3.0 * momentum[1] * weighted_total
    grad_mz = jnp.sum(vel_z * slope_terms, axis=0) - 3.0 * momentum[2] * weighted_total
    bounced = jnp.stack([solid_adj[k] for k in OPPOSITE], axis=0)
    grad_pops = (
        (1.0 - TAU_INV) * melt_adj
        + grad_noneq
        + grad_density
        + vel_x * grad_mx
        + vel_y * grad_my
        + vel_z * grad_mz
        + bounced
    )
    return (grad_pops, (grad_w_in, grad_b_in, grad_w_out))


def collide_field(field, flags, w_in, b_in, w_out):

    def collide_one_plane(inputs):
        plane, flag_plane = inputs
        result = collide_plane(
            plane.reshape(plane.shape[0], -1),
            flag_plane.reshape(-1).astype(jnp.float32),
            w_in,
            b_in,
            w_out,
        )
        return result.reshape(plane.shape)

    return lax.map(collide_one_plane, (field, flags))


def adjoint_field(field, flags, incoming, w_in, b_in, w_out):
    units = w_in.shape[0]
    width = w_in.shape[1]
    start = (
        jnp.zeros((units, width), jnp.float32),
        jnp.zeros((units,), jnp.float32),
        jnp.zeros((width, units), jnp.float32),
    )

    def adjoint_one_plane(carry, inputs):
        plane, flag_plane, grad_plane = inputs
        grad_pops, grads = adjoint_plane(
            plane.reshape(plane.shape[0], -1),
            flag_plane.reshape(-1).astype(jnp.float32),
            grad_plane.reshape(plane.shape[0], -1),
            w_in,
            b_in,
            w_out,
        )
        return (tuple((c + g for c, g in zip(carry, grads))), grad_pops.reshape(plane.shape))

    totals, grad_field = lax.scan(adjoint_one_plane, start, (field, flags, incoming))
    return (totals, grad_field)


def stream_local(field, sign):
    count_x = field.shape[0]
    count_y = field.shape[2]
    comps = []
    padded = padded_2(field, (("gx", 0), ("gy", 2)), 1)
    for comp in range(len(VELOCITY)):
        step_x, step_y, step_z = [sign * v for v in VELOCITY[comp]]
        piece = padded[
            1 - step_x : 1 - step_x + count_x, comp, 1 - step_y : 1 - step_y + count_y, :
        ]
        comps.append(jnp.roll(piece, step_z, axis=2))
    return jnp.stack(comps, axis=1)


def normalized(total):
    return total / jnp.sqrt(jnp.mean(total * total) + 1e-06)


def shards(populations, cotangent, flags, w_in, b_in, w_out):
    post = collide_field(populations, flags, w_in, b_in, w_out)
    shifted = stream_local(post, 1)
    incoming = stream_local(cotangent.astype(jnp.float32), -1)
    grads_late, back_late = adjoint_field(shifted, flags, incoming, w_in, b_in, w_out)
    before = stream_local(back_late, -1)
    grads_early, back_early = adjoint_field(populations, flags, before, w_in, b_in, w_out)
    merged = [a + b for a, b in zip(grads_early, grads_late)]
    totals = lax.psum((merged[0], merged[1], merged[2]), ("gx", "gy"))
    return (
        back_early.astype(jnp.bfloat16),
        normalized(totals[0]),
        normalized(totals[1]),
        normalized(totals[2]),
    )


def solution(mesh):
    placed = (
        P("gx", None, "gy", None),
        P("gx", None, "gy", None),
        P("gx", "gy", None),
        P(),
        P(),
        P(),
    )
    return jax.shard_map(
        shards,
        mesh=mesh,
        in_specs=placed,
        out_specs=(P("gx", None, "gy", None), P(), P(), P()),
        check_vma=False,
    )
```

profile of v0, /device:TPU:1, one launch (start us, length us, event | category | flops | bytes accessed | tf_op | source)
XLA Modules:
  0.0 318.5 jit_solution(5839086551487248528)
XLA Ops:
  0.7 14.5 %while.52 = (s32[]{:T(128)}, f32[2,19,16,256]{3,2,1,0:T(8,128)S(1)}, s32[2,16,256]{2,1,0:T(8,128)}, f32[2,19,16,256]{3,2,1,0:T(8,128)}, bf16[128,19]{0,1:T(8,128...) while((s32[]{:T(128)}, ...), condition=%wide.region_5.6_spmd.clone.clone, body=%wide.region_0.5_spmd.sunk.clone.clone.sunk | while | flops 44105748 | bytes 6781221 | solution.py:141
  5.7 2.0 fusion.148
  13.0 2.0 fusion.148
  16.0 4.9 %collective-permute-start.4 = (f32[1,19,16,256]{3,2,0,1:T(8,128)}, f32[1,19,16,256]{3,2,0,1:T(8,128)S(1)}, u32[]{:S(2)}, u32[]{:S(2)}) collective-permute-start(f32[1,19,16,256]{3,2,0,1:T(8,128)} %get-tuple-element.939), channel_id=1, source_target_pairs={{0,4},{4,8},{8,12},{12,16},{16,20},{20,24},{24,28},{28,32},{32,36}... | collective-permute-start | bytes 933896 | tf_op jit(solution)/shard_map/ppermute | solution.py:40
  20.9 5.7 %collective-permute-start.5 = (f32[1,19,16,256]{3,2,0,1:T(8,128)S(1)}, f32[1,19,16,256]{3,2,0,1:T(8,128)S(1)}, u32[]{:S(2)}, u32[]{:S(2)}) collective-permute-start(f32[1,19,16,256]{3,2,0,1:T(8,128)S(1)} %get-tuple-element.938), channel_id=1, source_target_pairs={{4,0},{8,4},{12,8},{16,12},{20,16},{24,20},{28,24},{32,28},{36,32}... | collective-permute-start | bytes 933896 | tf_op jit(solution)/shard_map/ppermute | solution.py:42
  26.8 7.9 %collective-permute-start = (f32[1,19,16,256]{3,2,0,1:T(8,128)S(1)}, f32[1,19,16,256]{3,2,0,1:T(8,128)S(1)}, u32[]{:S(2)}, u32[]{:S(2)}) collective-permute-start(f32[1,19,16,256]{3,2,0,1:T(8,128)S(1)} %get-tuple-element.944), channel_id=1, source_target_pairs={{4,0},{8,4},{12,8},{16,12},{20,16},{24,20},{28,24},{32,28},{36,32}... | collective-permute-start | bytes 933896 | tf_op jit(solution)/shard_map/ppermute | solution.py:42
  34.7 1.9 collective-permute-start.1
  42.1 3.1 collective-permute-start.6
  45.2 3.4 %collective-permute-start.7 = (f32[4,19,1,256]{3,2,0,1:T(1,128)S(1)}, f32[4,19,1,256]{3,2,0,1:T(1,128)S(1)}, u32[]{:S(2)}, u32[]{:S(2)}) collective-permute-start(f32[4,19,1,256]{3,2,0,1:T(1,128)S(1)} %get-tuple-element.909), channel_id=1, source_target_pairs={{1,0},{2,1},{3,2},{0,3},{5,4},{6,5},{7,6},{4,7},{9,8},{10,9},{11,1... | collective-permute-start | bytes 233480 | tf_op jit(solution)/shard_map/ppermute | solution.py:42
  48.8 3.2 collective-permute-start.2
  52.0 2.1 collective-permute-start.3
  55.6 2.7 collective-permute-done.3
  80.5 42.9 %while.53 = (s32[]{:T(128)}, f32[128,19]{0,1:T(8,128)}, f32[128]{0:T(128)}, f32[19,128]{1,0:T(8,128)}, f32[2,19,16,256]{3,2,1,0:T(8,128)}, /*index=5*/f32[2,19,1...) while((s32[]{:T(128)}, f32[128,19]{0,1:T(8,128)}, ...), condition=%wide.region_17.18_spmd.clone.clone.clone, body=%wide.region_6.17_spmd.sunk.clone.clone.clone.sunk | while | flops 109766272 | bytes 23366228 | solution.py:165
  81.2 1.3 multiply_reduce_fusion.26
  82.9 1.5 fusion.157
  85.1 1.3 convert_reduce_fusion.4
  86.4 2.2 fusion.159
  91.1 4.8 %stack.186 = f32[19,4096]{1,0:T(8,128)} concatenate(f32[1,4096]{1,0:T(1,128)} %get-tuple-element.1264, f32[1,4096]{1,0:T(1,128)} %get-tuple-element.1265, f32[1,4096]{1,0:T(1,128)} %get-tuple-element.1266, f32[1,4096]{1,0:T(1,128)} %get-tuple-element.1267, f32[1,4096]{1,0:T(1,128)} %get-tuple-element.1268, f32[1,4096]{1,0:T(1,128)} %get-tuple-element.1269, ...), dimensions={0} | concatenate | bytes 622592 | tf_op jit(solution)/shard_map/while/body/eval_jaxpr/stack | solution.py:115
  95.9 1.3 fusion.162
  98.1 2.1 convolution_add_fusion.11
  102.3 1.3 multiply_reduce_fusion.26
  104.0 1.5 fusion.157
  106.2 1.3 convert_reduce_fusion.4
  107.5 2.2 fusion.159
  112.2 4.8 %stack.186 = f32[19,4096]{1,0:T(8,128)} concatenate(f32[1,4096]{1,0:T(1,128)} %get-tuple-element.1264, f32[1,4096]{1,0:T(1,128)} %get-tuple-element.1265, f32[1,4096]{1,0:T(1,128)} %get-tuple-element.1266, f32[1,4096]{1,0:T(1,128)} %get-tuple-element.1267, f32[1,4096]{1,0:T(1,128)} %get-tuple-element.1268, f32[1,4096]{1,0:T(1,128)} %get-tuple-element.1269, ...), dimensions={0} | concatenate | bytes 622592 | tf_op jit(solution)/shard_map/while/body/eval_jaxpr/stack | solution.py:115
  117.0 1.3 fusion.162
  119.2 2.1 convolution_add_fusion.11
  121.8 1.6 convolution_add_fusion.12
  124.5 6.4 %collective-permute-start.9 = (f32[1,19,16,256]{3,2,0,1:T(8,128)S(1)}, f32[1,19,16,256]{3,2,0,1:T(8,128)S(1)}, u32[]{:S(2)}, u32[]{:S(2)}) collective-permute-start(f32[1,19,16,256]{3,2,0,1:T(8,128)S(1)} %get-tuple-element.931), channel_id=1, source_target_pairs={{0,4},{4,8},{8,12},{12,16},{16,20},{20,24},{24,28},{28,32},{32,36}... | collective-permute-start | bytes 933896 | tf_op jit(solution)/shard_map/ppermute | solution.py:40
  131.8 5.9 %collective-permute-start.8 = (f32[1,19,16,256]{3,2,0,1:T(8,128)S(1)}, f32[1,19,16,256]{3,2,0,1:T(8,128)S(1)}, u32[]{:S(2)}, u32[]{:S(2)}) collective-permute-start(f32[1,19,16,256]{3,2,0,1:T(8,128)S(1)} %get-tuple-element.932), channel_id=1, source_target_pairs={{4,0},{8,4},{12,8},{16,12},{20,16},{24,20},{28,24},{32,28},{36,32}... | collective-permute-start | bytes 933896 | tf_op jit(solution)/shard_map/ppermute | solution.py:42
  137.7 1.4 constant_dynamic-update-slice_fusion.70
  139.2 1.3 constant_dynamic-update-slice_fusion.50
  140.7 1.9 collective-permute-start.10
  142.6 3.5 %collective-permute-start.11 = (f32[4,19,1,256]{3,2,0,1:T(1,128)S(1)}, f32[4,19,1,256]{3,2,0,1:T(1,128)S(1)}, u32[]{:S(2)}, u32[]{:S(2)}) collective-permute-start(f32[4,19,1,256]{3,2,0,1:T(1,128)S(1)} %get-tuple-element.905), channel_id=1, source_target_pairs={{0,1},{1,2},{2,3},{3,0},{4,5},{5,6},{6,7},{7,4},{8,9},{9,10},{10,1... | collective-permute-start | bytes 233480 | tf_op jit(solution)/shard_map/ppermute | solution.py:40
  159.9 42.6 %while.54 = (s32[]{:T(128)}, f32[128,19]{0,1:T(8,128)}, f32[128]{0:T(128)}, f32[19,128]{1,0:T(8,128)}, bf16[2,19,16,256]{3,2,1,0:T(8,128)(2,1)}, /*index=5*/f32[...) while((s32[]{:T(128)}, f32[128,19]{0,1:T(8,128)}, ...), condition=%wide.region_29.30_spmd.clone.clone.clone, body=%wide.region_18.29_spmd.sunk.clone.clone.clone.sunk | while | flops 109844096 | bytes 22506068 | solution.py:165
  162.3 1.5 fusion.171
  164.6 1.3 convert_reduce_fusion.5
  165.8 2.2 fusion.173
  170.5 4.8 %stack.187 = f32[19,4096]{1,0:T(8,128)} concatenate(f32[1,4096]{1,0:T(1,128)} %get-tuple-element.1316, f32[1,4096]{1,0:T(1,128)} %get-tuple-element.1317, f32[1,4096]{1,0:T(1,128)} %get-tuple-element.1318, f32[1,4096]{1,0:T(1,128)} %get-tuple-element.1319, f32[1,4096]{1,0:T(1,128)} %get-tuple-element.1320, f32[1,4096]{1,0:T(1,128)} %get-tuple-element.1321, ...), dimensions={0} | concatenate | bytes 622592 | tf_op jit(solution)/shard_map/while/body/eval_jaxpr/stack | solution.py:115
  175.3 1.4 fusion.176
  177.4 2.1 convolution_add_fusion.13
  183.3 1.5 fusion.171
  186.8 2.2 fusion.173
  191.5 4.8 %stack.187 = f32[19,4096]{1,0:T(8,128)} concatenate(f32[1,4096]{1,0:T(1,128)} %get-tuple-element.1316, f32[1,4096]{1,0:T(1,128)} %get-tuple-element.1317, f32[1,4096]{1,0:T(1,128)} %get-tuple-element.1318, f32[1,4096]{1,0:T(1,128)} %get-tuple-element.1319, f32[1,4096]{1,0:T(1,128)} %get-tuple-element.1320, f32[1,4096]{1,0:T(1,128)} %get-tuple-element.1321, ...), dimensions={0} | concatenate | bytes 622592 | tf_op jit(solution)/shard_map/while/body/eval_jaxpr/stack | solution.py:115
  196.3 1.4 fusion.176
  198.4 2.1 convolution_add_fusion.13
  201.0 1.6 convolution_add_fusion.14
  204.6 108.2 %all-reduce = (f32[128,19]{0,1:T(8,128)S(1)}, f32[128]{0:T(128)S(1)}, f32[19,128]{1,0:T(8,128)S(1)}) all-reduce(f32[128,19]{0,1:T(8,128)S(1)} %add.296, f32[128]{0:T(128)S(1)} %add.298, f32[19,128]{1,0:T(8,128)S(1)} %add.300), channel_id=1, replica_groups=mesh['gx'=128,'gy'=4] {'gx','gy'}, use_global_device_ids=true, to_apply=%region_30.31 | all-reduce | flops 4992 | bytes 39936 | tf_op jit(solution)/shard_map/psum | solution.py:195
  (382 shorter events, 89.0 us)
Async XLA Ops:
  3.4 2.3 copy-start.12
  10.7 2.3 copy-start.12
  15.2 11.4 %copy-start.15 = (bf16[2,19,16,256]{3,2,1,0:T(8,128)(2,1)S(1)}, bf16[2,19,16,256]{3,2,1,0:T(8,128)(2,1)}, u32[]{:S(2)}) copy-start(bf16[2,19,16,256]{3,2,1,0:T(8,128)(2,1)} %param.38) | copy-start | bytes 933892
  16.0 22.8 %collective-permute-start.4 = (f32[1,19,16,256]{3,2,0,1:T(8,128)}, f32[1,19,16,256]{3,2,0,1:T(8,128)S(1)}, u32[]{:S(2)}, u32[]{:S(2)}) collective-permute-start(f32[1,19,16,256]{3,2,0,1:T(8,128)} %get-tuple-element.939), channel_id=1, source_target_pairs={{0,4},{4,8},{8,12},{12,16},{16,20},{20,24},{24,28},{28,32},{32,36}... | collective-permute-start | bytes 933896 | tf_op jit(solution)/shard_map/ppermute | solution.py:40
  20.9 18.2 %collective-permute-start.5 = (f32[1,19,16,256]{3,2,0,1:T(8,128)S(1)}, f32[1,19,16,256]{3,2,0,1:T(8,128)S(1)}, u32[]{:S(2)}, u32[]{:S(2)}) collective-permute-start(f32[1,19,16,256]{3,2,0,1:T(8,128)S(1)} %get-tuple-element.938), channel_id=1, source_target_pairs={{4,0},{8,4},{12,8},{16,12},{20,16},{24,20},{28,24},{32,28},{36,32}... | collective-permute-start | bytes 933896 | tf_op jit(solution)/shard_map/ppermute | solution.py:42
  26.8 12.6 %collective-permute-start = (f32[1,19,16,256]{3,2,0,1:T(8,128)S(1)}, f32[1,19,16,256]{3,2,0,1:T(8,128)S(1)}, u32[]{:S(2)}, u32[]{:S(2)}) collective-permute-start(f32[1,19,16,256]{3,2,0,1:T(8,128)S(1)} %get-tuple-element.944), channel_id=1, source_target_pairs={{4,0},{8,4},{12,8},{16,12},{20,16},{24,20},{28,24},{32,28},{36,32}... | collective-permute-start | bytes 933896 | tf_op jit(solution)/shard_map/ppermute | solution.py:42
  34.7 5.8 %collective-permute-start.1 = (f32[1,19,16,256]{3,2,0,1:T(8,128)S(1)}, f32[1,19,16,256]{3,2,0,1:T(8,128)S(1)}, u32[]{:S(2)}, u32[]{:S(2)}) collective-permute-start(f32[1,19,16,256]{3,2,0,1:T(8,128)S(1)} %get-tuple-element.943), channel_id=1, source_target_pairs={{0,4},{4,8},{8,12},{12,16},{16,20},{20,24},{24,28},{28,32},{32,36}... | collective-permute-start | bytes 933896 | tf_op jit(solution)/shard_map/ppermute | solution.py:40
  42.1 13.4 %collective-permute-start.6 = (f32[4,19,1,256]{3,2,0,1:T(1,128)S(1)}, f32[4,19,1,256]{3,2,0,1:T(1,128)S(1)}, u32[]{:S(2)}, u32[]{:S(2)}) collective-permute-start(f32[4,19,1,256]{3,2,0,1:T(1,128)S(1)} %get-tuple-element.910), channel_id=1, source_target_pairs={{0,1},{1,2},{2,3},{3,0},{4,5},{5,6},{6,7},{7,4},{8,9},{9,10},{10,1... | collective-permute-start | bytes 233480 | tf_op jit(solution)/shard_map/ppermute | solution.py:40
  45.2 10.2 %collective-permute-start.7 = (f32[4,19,1,256]{3,2,0,1:T(1,128)S(1)}, f32[4,19,1,256]{3,2,0,1:T(1,128)S(1)}, u32[]{:S(2)}, u32[]{:S(2)}) collective-permute-start(f32[4,19,1,256]{3,2,0,1:T(1,128)S(1)} %get-tuple-element.909), channel_id=1, source_target_pairs={{1,0},{2,1},{3,2},{0,3},{5,4},{6,5},{7,6},{4,7},{9,8},{10,9},{11,1... | collective-permute-start | bytes 233480 | tf_op jit(solution)/shard_map/ppermute | solution.py:42
  48.8 6.8 %collective-permute-start.2 = (f32[4,19,1,256]{3,2,0,1:T(1,128)S(1)}, f32[4,19,1,256]{3,2,0,1:T(1,128)S(1)}, u32[]{:S(2)}, u32[]{:S(2)}) collective-permute-start(f32[4,19,1,256]{3,2,0,1:T(1,128)S(1)} %get-tuple-element.914), channel_id=1, source_target_pairs={{1,0},{2,1},{3,2},{0,3},{5,4},{6,5},{7,6},{4,7},{9,8},{10,9},{11,1... | collective-permute-start | bytes 233480 | tf_op jit(solution)/shard_map/ppermute | solution.py:42
  52.0 6.4 %collective-permute-start.3 = (f32[4,19,1,256]{3,2,0,1:T(1,128)S(1)}, f32[4,19,1,256]{3,2,0,1:T(1,128)S(1)}, u32[]{:S(2)}, u32[]{:S(2)}) collective-permute-start(f32[4,19,1,256]{3,2,0,1:T(1,128)S(1)} %get-tuple-element.913), channel_id=1, source_target_pairs={{0,1},{1,2},{2,3},{3,0},{4,5},{5,6},{6,7},{7,4},{8,9},{9,10},{10,1... | collective-permute-start | bytes 233480 | tf_op jit(solution)/shard_map/ppermute | solution.py:40
  82.5 7.1 %copy-start.2 = (f32[2,2,8,128]{3,1,2,0:T(2,128)}, f32[2,2,8,128]{3,1,2,0:T(2,128)S(1)}, u32[]{:S(2)}) copy-start(f32[2,2,8,128]{3,1,2,0:T(2,128)S(1)} %copy.221) | copy-start | bytes 49156 | tf_op jit(solution)/shard_map/while
  82.5 7.0 %copy-start.4 = (f32[2,2,8,128]{3,1,2,0:T(2,128)}, f32[2,2,8,128]{3,1,2,0:T(2,128)S(1)}, u32[]{:S(2)}) copy-start(f32[2,2,8,128]{3,1,2,0:T(2,128)S(1)} %copy.222) | copy-start | bytes 49156 | tf_op jit(solution)/shard_map/while
  82.5 7.0 %copy-start.6 = (f32[2,2,8,128]{3,1,2,0:T(2,128)}, f32[2,2,8,128]{3,1,2,0:T(2,128)S(1)}, u32[]{:S(2)}) copy-start(f32[2,2,8,128]{3,1,2,0:T(2,128)S(1)} %copy.223) | copy-start | bytes 49156 | tf_op jit(solution)/shard_map/while
  82.6 1.8 copy-start.10
  82.8 1.6 copy-start
  82.9 1.5 copy-start.8
  84.4 0.7 copy-start.13
  98.1 2.1 copy-start.16
  98.1 2.1 copy-start.20
  103.6 7.1 %copy-start.2 = (f32[2,2,8,128]{3,1,2,0:T(2,128)}, f32[2,2,8,128]{3,1,2,0:T(2,128)S(1)}, u32[]{:S(2)}) copy-start(f32[2,2,8,128]{3,1,2,0:T(2,128)S(1)} %copy.221) | copy-start | bytes 49156 | tf_op jit(solution)/shard_map/while
  103.6 7.0 %copy-start.4 = (f32[2,2,8,128]{3,1,2,0:T(2,128)}, f32[2,2,8,128]{3,1,2,0:T(2,128)S(1)}, u32[]{:S(2)}) copy-start(f32[2,2,8,128]{3,1,2,0:T(2,128)S(1)} %copy.222) | copy-start | bytes 49156 | tf_op jit(solution)/shard_map/while
  103.6 7.0 %copy-start.6 = (f32[2,2,8,128]{3,1,2,0:T(2,128)}, f32[2,2,8,128]{3,1,2,0:T(2,128)S(1)}, u32[]{:S(2)}) copy-start(f32[2,2,8,128]{3,1,2,0:T(2,128)S(1)} %copy.223) | copy-start | bytes 49156 | tf_op jit(solution)/shard_map/while
  103.7 1.8 copy-start.10
  104.0 1.6 copy-start
  104.0 1.5 copy-start.8
  119.2 2.1 copy-start.16
  119.2 2.1 copy-start.20
  124.5 14.6 %collective-permute-start.9 = (f32[1,19,16,256]{3,2,0,1:T(8,128)S(1)}, f32[1,19,16,256]{3,2,0,1:T(8,128)S(1)}, u32[]{:S(2)}, u32[]{:S(2)}) collective-permute-start(f32[1,19,16,256]{3,2,0,1:T(8,128)S(1)} %get-tuple-element.931), channel_id=1, source_target_pairs={{0,4},{4,8},{8,12},{12,16},{16,20},{20,24},{24,28},{28,32},{32,36}... | collective-permute-start | bytes 933896 | tf_op jit(solution)/shard_map/ppermute | solution.py:40
  131.8 8.7 %collective-permute-start.8 = (f32[1,19,16,256]{3,2,0,1:T(8,128)S(1)}, f32[1,19,16,256]{3,2,0,1:T(8,128)S(1)}, u32[]{:S(2)}, u32[]{:S(2)}) collective-permute-start(f32[1,19,16,256]{3,2,0,1:T(8,128)S(1)} %get-tuple-element.932), channel_id=1, source_target_pairs={{4,0},{8,4},{12,8},{16,12},{20,16},{24,20},{28,24},{32,28},{36,32}... | collective-permute-start | bytes 933896 | tf_op jit(solution)/shard_map/ppermute | solution.py:42
  140.7 7.0 %collective-permute-start.10 = (f32[4,19,1,256]{3,2,0,1:T(1,128)S(1)}, f32[4,19,1,256]{3,2,0,1:T(1,128)S(1)}, u32[]{:S(2)}, u32[]{:S(2)}) collective-permute-start(f32[4,19,1,256]{3,2,0,1:T(1,128)S(1)} %get-tuple-element.906), channel_id=1, source_target_pairs={{1,0},{2,1},{3,2},{0,3},{5,4},{6,5},{7,6},{4,7},{9,8},{10,9},{11,1... | collective-permute-start | bytes 233480 | tf_op jit(solution)/shard_map/ppermute | solution.py:42
  142.6 6.4 %collective-permute-start.11 = (f32[4,19,1,256]{3,2,0,1:T(1,128)S(1)}, f32[4,19,1,256]{3,2,0,1:T(1,128)S(1)}, u32[]{:S(2)}, u32[]{:S(2)}) collective-permute-start(f32[4,19,1,256]{3,2,0,1:T(1,128)S(1)} %get-tuple-element.905), channel_id=1, source_target_pairs={{0,1},{1,2},{2,3},{3,0},{4,5},{5,6},{6,7},{7,4},{8,9},{9,10},{10,1... | collective-permute-start | bytes 233480 | tf_op jit(solution)/shard_map/ppermute | solution.py:40
  161.9 7.0 %copy-start.3 = (f32[2,2,8,128]{3,1,2,0:T(2,128)}, f32[2,2,8,128]{3,1,2,0:T(2,128)S(1)}, u32[]{:S(2)}) copy-start(f32[2,2,8,128]{3,1,2,0:T(2,128)S(1)} %copy.230) | copy-start | bytes 49156 | tf_op jit(solution)/shard_map/while
  162.0 7.0 %copy-start.5 = (f32[2,2,8,128]{3,1,2,0:T(2,128)}, f32[2,2,8,128]{3,1,2,0:T(2,128)S(1)}, u32[]{:S(2)}) copy-start(f32[2,2,8,128]{3,1,2,0:T(2,128)S(1)} %copy.231) | copy-start | bytes 49156 | tf_op jit(solution)/shard_map/while
  162.0 7.0 %copy-start.7 = (f32[2,2,8,128]{3,1,2,0:T(2,128)}, f32[2,2,8,128]{3,1,2,0:T(2,128)S(1)}, u32[]{:S(2)}) copy-start(f32[2,2,8,128]{3,1,2,0:T(2,128)S(1)} %copy.232) | copy-start | bytes 49156 | tf_op jit(solution)/shard_map/while
  162.0 1.8 copy-start.11
  162.3 1.6 copy-start.1
  162.3 1.5 copy-start.9
  177.4 2.1 copy-start.17
  177.4 2.1 copy-start.18
  182.9 7.0 %copy-start.3 = (f32[2,2,8,128]{3,1,2,0:T(2,128)}, f32[2,2,8,128]{3,1,2,0:T(2,128)S(1)}, u32[]{:S(2)}) copy-start(f32[2,2,8,128]{3,1,2,0:T(2,128)S(1)} %copy.230) | copy-start | bytes 49156 | tf_op jit(solution)/shard_map/while
  182.9 7.0 %copy-start.5 = (f32[2,2,8,128]{3,1,2,0:T(2,128)}, f32[2,2,8,128]{3,1,2,0:T(2,128)S(1)}, u32[]{:S(2)}) copy-start(f32[2,2,8,128]{3,1,2,0:T(2,128)S(1)} %copy.231) | copy-start | bytes 49156 | tf_op jit(solution)/shard_map/while
  183.0 7.0 %copy-start.7 = (f32[2,2,8,128]{3,1,2,0:T(2,128)}, f32[2,2,8,128]{3,1,2,0:T(2,128)S(1)}, u32[]{:S(2)}) copy-start(f32[2,2,8,128]{3,1,2,0:T(2,128)S(1)} %copy.232) | copy-start | bytes 49156 | tf_op jit(solution)/shard_map/while
  183.0 1.8 copy-start.11
  183.3 1.6 copy-start.1
  183.3 1.5 copy-start.9
  198.4 2.1 copy-start.17
  198.4 2.1 copy-start.18
  (7 other events, 4.0 us)
where the time goes:
time: 323 us; the launch traced here: 318 us
  blocking collectives  108 us (33%)
  other arithmetic  62.4 us (19%)
  local copies, waits for them, and re-layouts  51.1 us (16%)
  starting transfers between devices  50 us (15%)
  matrix products  37.1 us (11%)
  waiting for transfers between devices  5.09 us (2%)
    psum x1, blocking collectives, shards(): totals = lax.psum((merged[0], merged[1], merged[2]), ('gx', 'gy'))  108 us
    unnamed x54, other arithmetic  31.7 us
    ppermute x6, starting transfers between devices, padded_2(): lax.ppermute(head, axis, [((i + 1) % count, i) for i in range(count)])  28.1 us
    ppermute x6, starting transfers between devices, padded_2(): lax.ppermute(tail, axis, [(i, (i + 1) % count) for i in range(count)])  22 us
    another operation x4, local copies, waits for them, and re-layouts, adjoint_plane(): bounced = jnp.stack([solid_adj[k] for k in OPPOSITE], axis=0)  19.2 us
    while x184, local copies, waits for them, and re-layouts  11.4 us
    dot_general x4, matrix products, adjoint_plane(): jnp.dot(w_in.T, grad_preact, preferred_element_type=jnp.float32) / weights  8.67 us
    dot_general x4, matrix products, adjoint_plane(): lax.dot_general(grad_preact, features, contract, preferred_element_type=j...  8.26 us
  transfers between devices with their start and end apart: 12, of which 3 were waited for; matrix products, arithmetic and copies ran while one was open for 3% of the time, Pallas kernels for 0%

commit v1 on v0

v1 whole, which is shorter than its diff:
```python
import functools

import jax
import jax.numpy as jnp
from jax import lax
from jax.experimental import pallas as pl
from jax.experimental.pallas import tpu as pltpu
from jax.sharding import PartitionSpec as P

VELOCITY = [
    (0, 0, 0),
    (1, 0, 0),
    (-1, 0, 0),
    (0, 1, 0),
    (0, -1, 0),
    (0, 0, 1),
    (0, 0, -1),
    (1, 1, 0),
    (-1, -1, 0),
    (1, -1, 0),
    (-1, 1, 0),
    (1, 0, 1),
    (-1, 0, -1),
    (1, 0, -1),
    (-1, 0, 1),
    (0, 1, 1),
    (0, -1, -1),
    (0, 1, -1),
    (0, -1, 1),
]
OPPOSITE = [0, 2, 1, 4, 3, 6, 5, 8, 7, 10, 9, 12, 11, 14, 13, 16, 15, 18, 17]
INV_W = [3.0] + [18.0] * 6 + [36.0] * 12
W = [1.0 / 3.0] + [1.0 / 18.0] * 6 + [1.0 / 36.0] * 12
PAIRS = [(i, i + 1) for i in range(1, 19, 2)]
Q = 19
UNITS = 128
ROWS = 160
DEPTH = 256
HID = 8 * UNITS
LANES = 256
GROUPS = 4

X_PLUS = [1, 7, 9, 11, 13]
X_MINUS = [2, 8, 10, 12, 14]
Y_PLUS = [(3, 0), (3, 1), (15, 0), (15, 1), (17, 0), (17, 1), (7, 0), (10, 1)]
Y_MINUS = [(4, 0), (4, 1), (16, 0), (16, 1), (18, 0), (18, 1), (9, 0), (8, 1)]
CORNERS = [7, 10, 8, 9]
MESH = pl.DeviceIdType.MESH
BF = jnp.bfloat16
F32 = jnp.float32
NT = (((1,), (1,)), ((), ()))
TN = (((0,), (0,)), ((), ()))


class Exchange:
    def __init__(self, refs):
        (self.own, self.sxp, self.sxm, self.syp, self.sym, self.rxl, self.rxr,
         self.ryl, self.ryu, self.rc, self.send, self.recv) = refs

    def put(self, j, p, s, val):
        cx, cy, cz = VELOCITY[j]
        if cz:
            val = pltpu.roll(val, cz % LANES, 1)
        rows = pl.ds(8 * s, 8)
        if cx == 1 and p == 1:
            self.sxp[X_PLUS.index(j), rows, :] = val
        elif cx == -1 and p == 0:
            self.sxm[X_MINUS.index(j), rows, :] = val
        else:
            self.own[p, j, rows, :] = val
        if cy == 1 and s == 1 and (j, p) in Y_PLUS:
            k = Y_PLUS.index((j, p))
            self.syp[k : k + 1, :] = val[7:8, :]
        if cy == -1 and s == 0 and (j, p) in Y_MINUS:
            k = Y_MINUS.index((j, p))
            self.sym[k : k + 1, :] = val[0:1, :]

    def copies(self, gx, gy):
        xr, xl = lax.rem(gx + 1, 128), lax.rem(gx + 127, 128)
        yu, yd = lax.rem(gy + 1, 4), lax.rem(gy + 3, 4)
        plan = [
            (self.sxp.at[:, :, :], self.rxl.at[:, :, :], (xr, gy)),
            (self.sxm.at[:, :, :], self.rxr.at[:, :, :], (xl, gy)),
            (self.syp.at[:, :], self.ryl.at[:, :], (gx, yu)),
            (self.sym.at[:, :], self.ryu.at[:, :], (gx, yd)),
            (self.sxp.at[1, pl.ds(8, 8), :], self.rc.at[0], (xr, yu)),
            (self.sxm.at[2, pl.ds(8, 8), :], self.rc.at[1], (xl, yu)),
            (self.sxm.at[1, pl.ds(0, 8), :], self.rc.at[2], (xl, yd)),
            (self.sxp.at[2, pl.ds(0, 8), :], self.rc.at[3], (xr, yd)),
        ]
        return [
            pltpu.make_async_remote_copy(
                src_ref=src, dst_ref=dst, send_sem=self.send.at[k], recv_sem=self.recv.at[k],
                device_id=dev, device_id_type=MESH,
            )
            for k, (src, dst, dev) in enumerate(plan)
        ]

    def get(self, j, p, s):
        cx, cy, cz = VELOCITY[j]
        q = p - cx
        if q == -1:
            src = self.rxl.at[X_PLUS.index(j)]
        elif q == 2:
            src = self.rxr.at[X_MINUS.index(j)]
        else:
            src = self.own.at[q, j]
        if cy == 0:
            return src[8 * s : 8 * s + 8, :]
        row = lax.broadcasted_iota(jnp.int32, (8, LANES), 0)
        if cy == 1:
            if s == 1:
                return src[7:15, :]
            if q in (0, 1):
                k = Y_PLUS.index((j, q))
                halo = self.ryl[k : k + 1, :]
            else:
                halo = self.rc[CORNERS.index(j), 7:8, :]
            return jnp.where(row == 0, halo, pltpu.roll(src[0:8, :], 1, 0))
        if s == 0:
            return src[1:9, :]
        if q in (0, 1):
            k = Y_MINUS.index((j, q))
            halo = self.ryu[k : k + 1, :]
        else:
            halo = self.rc[CORNERS.index(j), 0:1, :]
        return jnp.where(row == 7, halo, pltpu.roll(src[8:16, :], 7, 0))


EX_SCRATCH = [
    pltpu.VMEM((2, Q, 16, LANES), F32),
    pltpu.VMEM((5, 16, LANES), F32),
    pltpu.VMEM((5, 16, LANES), F32),
    pltpu.VMEM((8, LANES), F32),
    pltpu.VMEM((8, LANES), F32),
    pltpu.VMEM((5, 16, LANES), F32),
    pltpu.VMEM((5, 16, LANES), F32),
    pltpu.VMEM((8, LANES), F32),
    pltpu.VMEM((8, LANES), F32),
    pltpu.VMEM((4, 8, LANES), F32),
    pltpu.SemaphoreType.DMA((8,)),
    pltpu.SemaphoreType.DMA((8,)),
]
N_EX = len(EX_SCRATCH)


def dot(a, b, dims=None):
    if dims is None:
        return jnp.dot(a, b, preferred_element_type=F32)
    return lax.dot_general(a, b, dims, preferred_element_type=F32)


def moments(f):
    rho = f[0]
    for a, b in PAIRS:
        rho = rho + (f[a] + f[b])
    mom = []
    for d in range(3):
        acc = None
        for a, b in PAIRS:
            c = VELOCITY[a][d]
            if c == 0:
                continue
            diff = f[a] - f[b] if c == 1 else f[b] - f[a]
            acc = diff if acc is None else acc + diff
        mom.append(acc)
    return rho, mom


def along(i, vec):
    out = None
    for d in range(3):
        c = VELOCITY[i][d]
        if c == 0:
            continue
        if out is None:
            out = vec[d] if c == 1 else -vec[d]
        else:
            out = out + vec[d] if c == 1 else out - vec[d]
    return out


def equilibrium(rho, mom):
    base = rho - 1.5 * (mom[0] * mom[0] + mom[1] * mom[1] + mom[2] * mom[2])
    eq = [base]
    for a, b in PAIRS:
        u = along(a, mom)
        even = base + 4.5 * (u * u)
        odd = 3.0 * u
        eq.append(even + odd)
        eq.append(even - odd)
    return eq


def store_features(dst, lanes, vals):
    for k in range(0, len(vals), 2):
        two = jnp.concatenate([vals[k], vals[k + 1]], axis=0)
        dst[8 * k : 8 * k + 16, lanes] = two.astype(BF)


def build_weights(w_in, b_in, w_out, w1, w1t, w2, w2t):
    comp_of = lax.broadcasted_iota(jnp.int32, (Q, DEPTH), 1) // 8
    expand = (lax.broadcasted_iota(jnp.int32, (Q, DEPTH), 0) == comp_of).astype(F32).astype(BF)
    comp_of_t = lax.broadcasted_iota(jnp.int32, (ROWS, Q), 0) // 8
    expand_t = (lax.broadcasted_iota(jnp.int32, (ROWS, Q), 1) == comp_of_t).astype(F32).astype(BF)
    hi = b_in[...].astype(BF)
    rest = b_in[...] - hi.astype(F32)
    mid = rest.astype(BF)
    low = (rest - mid.astype(F32)).astype(BF)
    row = lax.broadcasted_iota(jnp.int32, (8, UNITS), 0)
    parts = jnp.where(
        row == 0, hi.astype(F32),
        jnp.where(row == 1, mid.astype(F32), jnp.where(row == 2, low.astype(F32), 0.0)),
    ).astype(BF)
    place = (
        lax.broadcasted_iota(jnp.int32, (8, DEPTH), 1)
        == lax.broadcasted_iota(jnp.int32, (8, DEPTH), 0) + 8 * Q
    ).astype(F32).astype(BF)
    in_rep = dot(w_in[...], expand)
    bias_rep = dot(parts, place, TN)
    out_rep = dot(w_out[...], expand, TN)
    in_rep_t = dot(expand_t, w_in[...], NT)
    out_rep_t = dot(expand_t, w_out[...])
    lane = lax.broadcasted_iota(jnp.int32, (UNITS, DEPTH), 1) % 8
    sub = lax.broadcasted_iota(jnp.int32, (ROWS, UNITS), 0) % 8
    for y in range(8):
        block = pl.ds(UNITS * y, UNITS)
        w1[block, :] = (jnp.where(lane == y, in_rep, 0.0) + bias_rep).astype(BF)
        w2t[block, :] = jnp.where(lane == y, out_rep, 0.0).astype(BF)
        w1t[:, block] = jnp.where(sub == y, in_rep_t, 0.0).astype(BF)
        w2[:, block] = jnp.where(sub == y, out_rep_t, 0.0).astype(BF)


def kernel(pops, cot, flags, w_in, b_in, w_out, d0_ref, grads_ref, *scratch):
    gx, gy = lax.axis_index("gx"), lax.axis_index("gy")
    ex_c = Exchange(scratch[:N_EX])
    ex_p = Exchange(scratch[N_EX : 2 * N_EX])
    ex_d = Exchange(scratch[2 * N_EX : 3 * N_EX])
    (w1, w1t, w2, w2t, feat0, feat1, qa, qb, hid0, hid1, ra, rb, t0, t1, gh, field, grad,
     mom0, post) = scratch[3 * N_EX :]

    barrier = pltpu.get_barrier_semaphore()
    for dx in (1, 0, 127):
        for dy in (1, 0, 3):
            if dx == 0 and dy == 0:
                continue
            pl.semaphore_signal(
                barrier, inc=1,
                device_id=(lax.rem(gx + dx, 128), lax.rem(gy + dy, 4)), device_id_type=MESH,
            )

    for p in range(2):
        for i in range(Q):
            wide = cot[p, i].astype(F32)
            for s in range(2):
                ex_c.put(OPPOSITE[i], p, s, wide[8 * s : 8 * s + 8, :])
    build_weights(w_in, b_in, w_out, w1, w1t, w2, w2t)
    zero = jnp.zeros((DEPTH - ROWS, GROUPS * LANES), BF)
    for ref in (feat0, feat1, qa, qb):
        ref[ROWS:, :] = zero
    pl.semaphore_wait(barrier, 8)
    copies_c = ex_c.copies(gx, gy)
    for c in copies_c:
        c.start()

    one = jnp.ones((8, LANES), F32)
    nil = jnp.zeros((8, LANES), F32)

    def lanes_of(g):
        return pl.ds(pl.multiple_of(g * LANES, LANES), LANES)

    def melt_of(g):
        rows = pl.ds(pl.multiple_of((g % 2) * 8, 8), 8)
        return flags[g // 2, rows, :].astype(F32)

    def front(f, g, feat, hid, act):
        rho, mom = moments(f)
        eq = equilibrium(rho, mom)
        lanes = lanes_of(g)
        store_features(feat, lanes, [f[i] * INV_W[i] - eq[i] for i in range(Q)] + [one])
        for c in range(4):
            block = pl.ds(256 * c, 256)
            t = jnp.tanh(dot(w1[block, :], feat[:, lanes]))
            act[block, lanes] = t
            hid[block, lanes] = t.astype(BF)
        return rho, mom, eq

    def step_a(g, carry):
        p = g // 2
        rows = pl.ds(pl.multiple_of((g % 2) * 8, 8), 8)
        lanes = lanes_of(g)
        f = [pops[p, i, rows, :] for i in range(Q)]
        rho, mom, eq = front(f, g, feat0, hid0, t0)
        for d in range(3):
            mom0[g, d] = mom[d]
        learned = dot(w2[...], hid0[:, lanes])
        melt = melt_of(g) > 0.5
        excess = rho - 1.0
        for i in range(Q):
            val = -0.25 * f[i] + (1.25 * W[i]) * eq[i] + learned[8 * i : 8 * i + 8, :]
            cz = VELOCITY[i][2]
            if cz:
                val = val + (0.15 * W[i] * cz) * excess
            post[g, i] = jnp.where(melt, val, f[OPPOSITE[i]])
        return carry

    lax.fori_loop(0, GROUPS, step_a, 0)

    for g in range(GROUPS):
        for i in range(Q):
            ex_p.put(i, g // 2, g % 2, post[g, i])
    copies_p = ex_p.copies(gx, gy)
    for c in copies_p:
        c.start()

    for c in copies_c:
        c.wait()
    for g in range(GROUPS):
        for i in range(Q):
            grad[g, i] = ex_c.get(OPPOSITE[i], g // 2, g % 2)

    def hidden_grad(g, q):
        melt = melt_of(g)
        lanes = lanes_of(g)
        m = [grad[g, i] * melt for i in range(Q)]
        store_features(q, lanes, m + [nil])
        for c in range(4):
            block = pl.ds(256 * c, 256)
            gh[block, lanes] = dot(w2t[block, :], q[:, lanes])

    def step_q(g, carry):
        hidden_grad(g, qb)
        return carry

    lax.fori_loop(0, GROUPS, step_q, 0)

    for c in copies_p:
        c.wait()
    for g in range(GROUPS):
        for i in range(Q):
            field[g, i] = ex_p.get(i, g // 2, g % 2)

    def back(g, mom, act, r, put):
        lanes = lanes_of(g)
        melt = melt_of(g)
        for c in range(4):
            block = pl.ds(256 * c, 256)
            t = act[block, lanes]
            r[block, lanes] = (gh[block, lanes] * (1.0 - t * t)).astype(BF)
        prod = dot(w1t[...], r[:, lanes])
        m, wd = [], []
        for i in range(Q):
            m.append(grad[g, i] * melt)
            wd.append((1.25 * W[i]) * m[i] - prod[8 * i : 8 * i + 8, :])
        total = wd[0]
        lift = None
        dj = [None, None, None]
        for a, b in PAIRS:
            both = wd[a] + wd[b]
            total = total + both
            cz = VELOCITY[a][2]
            if cz:
                term = (0.15 * W[a] * cz) * (m[a] - m[b])
                lift = term if lift is None else lift + term
            slope = 3.0 * (wd[a] - wd[b]) + 9.0 * along(a, mom) * both
            for d in range(3):
                c = VELOCITY[a][d]
                if c == 0:
                    continue
                if dj[d] is None:
                    dj[d] = slope if c == 1 else -slope
                else:
                    dj[d] = dj[d] + slope if c == 1 else dj[d] - slope
        drho = total + lift
        dj = [dj[d] - 3.0 * mom[d] * total for d in range(3)]
        for i in range(Q):
            o = OPPOSITE[i]
            val = (-0.25) * m[i] + INV_W[i] * prod[8 * i : 8 * i + 8, :] + drho
            if i:
                val = val + along(i, dj)
            put(i, val + (grad[g, o] - m[o]))

    def step_b(g, carry):
        f = [field[g, i] for i in range(Q)]
        rho, mom, eq = front(f, g, feat1, hid1, t1)

        def put(i, val):
            post[g, i] = val

        back(g, mom, t1, rb, put)
        return carry

    lax.fori_loop(0, GROUPS, step_b, 0)
    for g in range(GROUPS):
        for i in range(Q):
            ex_d.put(OPPOSITE[i], g // 2, g % 2, post[g, i])
    copies_d = ex_d.copies(gx, gy)
    for c in copies_d:
        c.start()

    acc_out = dot(qb[:ROWS, :], hid1[...], NT)
    acc_in = dot(feat1[:ROWS, :], rb[...], NT)

    for c in copies_d:
        c.wait()
    for g in range(GROUPS):
        for i in range(Q):
            grad[g, i] = ex_d.get(OPPOSITE[i], g // 2, g % 2)

    def step_c(g, carry):
        hidden_grad(g, qa)
        p = g // 2
        rows = pl.ds(pl.multiple_of((g % 2) * 8, 8), 8)

        def put(i, val):
            d0_ref[p, i, rows, :] = val

        back(g, [mom0[g, d] for d in range(3)], t0, ra, put)
        return carry

    lax.fori_loop(0, GROUPS, step_c, 0)
    acc_out = acc_out + dot(qa[:ROWS, :], hid0[...], NT)
    acc_in = acc_in + dot(feat0[:ROWS, :], ra[...], NT)
    sub = lax.broadcasted_iota(jnp.int32, (ROWS, UNITS), 0) % 8
    for k, acc in enumerate((acc_in, acc_out)):
        tot = jnp.zeros((ROWS, UNITS), F32)
        for y in range(8):
            tot = tot + jnp.where(sub == y, acc[:, UNITS * y : UNITS * (y + 1)], 0.0)
        grads_ref[k] = jnp.sum(tot.reshape(20, 8, UNITS), axis=1)


def local_step(populations, cotangent, flags, w_in, b_in, w_out):
    vmem = pl.BlockSpec(memory_space=pltpu.VMEM)
    cells = GROUPS * LANES
    return pl.pallas_call(
        kernel,
        out_shape=(
            jax.ShapeDtypeStruct((2, Q, 16, LANES), F32),
            jax.ShapeDtypeStruct((2, 20, UNITS), F32),
        ),
        in_specs=[vmem] * 6,
        out_specs=(vmem, vmem),
        scratch_shapes=EX_SCRATCH * 3
        + [
            pltpu.VMEM((HID, DEPTH), BF),
            pltpu.VMEM((ROWS, HID), BF),
            pltpu.VMEM((ROWS, HID), BF),
            pltpu.VMEM((HID, DEPTH), BF),
            pltpu.VMEM((DEPTH, cells), BF),
            pltpu.VMEM((DEPTH, cells), BF),
            pltpu.VMEM((DEPTH, cells), BF),
            pltpu.VMEM((DEPTH, cells), BF),
            pltpu.VMEM((HID, cells), BF),
            pltpu.VMEM((HID, cells), BF),
            pltpu.VMEM((HID, cells), BF),
            pltpu.VMEM((HID, cells), BF),
            pltpu.VMEM((HID, cells), F32),
            pltpu.VMEM((HID, cells), F32),
            pltpu.VMEM((HID, cells), F32),
            pltpu.VMEM((GROUPS, Q, 8, LANES), F32),
            pltpu.VMEM((GROUPS, Q, 8, LANES), F32),
            pltpu.VMEM((GROUPS, 3, 8, LANES), F32),
            pltpu.VMEM((GROUPS, Q, 8, LANES), F32),
        ],
        compiler_params=pltpu.CompilerParams(
            collective_id=0, has_side_effects=True, vmem_limit_bytes=60 * 1024 * 1024
        ),
    )(populations, cotangent, flags, w_in, b_in.reshape(1, UNITS), w_out)


def normalized(total):
    return total / jnp.sqrt(jnp.mean(total * total) + 1e-06)


def shards(populations, cotangent, flags, w_in, b_in, w_out):
    d0, grads = local_step(populations, cotangent, flags, w_in, b_in, w_out)
    totals = lax.psum(grads, ("gx", "gy"))
    return (
        d0.astype(BF),
        normalized(totals[0, :Q].T),
        normalized(totals[0, Q]),
        normalized(totals[1, :Q]),
    )


def solution(mesh):
    placed = (
        P("gx", None, "gy", None),
        P("gx", None, "gy", None),
        P("gx", "gy", None),
        P(),
        P(),
        P(),
    )
    return jax.shard_map(
        shards,
        mesh=mesh,
        in_specs=placed,
        out_specs=(P("gx", None, "gy", None), P(), P(), P()),
        check_vma=False,
    )
```

time: 323 us -> 146 us (0.45); the launches traced: 318 us -> 146 us
  other arithmetic: 62.4 us -> 4.17 us
  starting transfers between devices: 50 us -> 0 us
  local copies, waits for them, and re-layouts: 51.1 us -> 1.42 us
  matrix products: 37.1 us -> 0 us
  Pallas kernels: 0 us -> 35.6 us
  blocking collectives: 108 us -> 102 us
  waiting for transfers between devices: 5.09 us -> 0 us
    ppermute x12 -> x0, starting transfers between devices: 50 us -> none  [the longest x6 28.1 us: padded_2(): lax.ppermute(head, axis, [((i + 1) % count, i) for i in range(count)])]
    dot_general x22 -> x0, matrix products: 37.1 us -> none  [the longest x4 8.67 us: adjoint_plane(): jnp.dot(w_in.T, grad_preact, preferred_element_type=jnp.float32) / weights]
    pallas_call x0 -> x1, Pallas kernels: none -> 35.6 us  [local_step(): pl.pallas_call(kernel, out_shape=(jax.ShapeDtypeStruct((2, Q, 16, LANES),...]
    unnamed x54 -> x0, other arithmetic: 31.7 us -> none
    another operation x8 -> x0, local copies, waits for them, and re-layouts: 21.1 us -> none  [the longest x4 19.2 us: adjoint_plane(): bounced = jnp.stack([solid_adj[k] for k in OPPOSITE], axis=0)]
    while x184 -> x0, local copies, waits for them, and re-layouts: 11.4 us -> none
    reduce_sum x10 -> x0, other arithmetic: 11 us -> none  [the longest x4 5.06 us: adjoint_plane(): grad_density = jnp.sum(weighted, axis=0) + jnp.sum(lift * melt_adj, axis=0)]
    add x15 -> x0, other arithmetic: 10 us -> none  [the longest x4 5.39 us: adjoint_plane(): (1.0 - TAU_INV) * melt_adj + grad_noneq + grad_density + vel_x * grad_mx]
  transfers between devices with their start and end apart: 12 -> 0, of which waited for: 3 -> 0; matrix products, arithmetic and copies ran while one was open for 3% -> 0% of each run, Pallas kernels for 0% -> 0%
where the time goes in v1:
time: 146 us
  blocking collectives  102 us (70%)
  Pallas kernels  35.6 us (24%)
  other arithmetic  4.17 us (3%)
  between operations  2.73 us (2%)
    psum x1, blocking collectives, shards(): totals = lax.psum(grads, ('gx', 'gy'))  102 us
    pallas_call x1, Pallas kernels, local_step(): pl.pallas_call(kernel, out_shape=(jax.ShapeDtypeStruct((2, Q, 16, LANES),...  35.6 us

profile of v1, /device:TPU:1, one launch (start us, length us, event | category | flops | bytes accessed | tf_op | source)
XLA Modules:
  0.0 146.1 jit_solution(3492517984989555719)
XLA Ops:
  0.6 1.4 copy.10.w_in
  2.0 35.6 %shard_map.93 = (f32[2,19,16,256]{3,2,1,0:T(8,128)}, f32[2,20,128]{2,1,0:T(8,128)}) custom-call(f32[2,19,16,256]{3,2,1,0:T(8,128)} %pops.1, bf16[2,19,16,256]{3,2,1,0:T(8,128)(2,1)} %cot.1, s32[2,16,256]{2,1,0:T(8,128)} %flags.1, bf16[128,19]{1,0:T(8,128)(2,1)} %copy.10.w_in, f32[1,128]{1,0:T(1,128)} %bitcast.9, bf16[19,128]{1,0:T(8,128)(2,1)} %w_out.1), custom_call_target="tpu_custom_call" | custom-call | tf_op jit(solution)/shard_map/pallas_call | solution.py:435
  37.7 0.0 copy-start
  37.7 1.8 %convert_element_type.3 = bf16[2,19,16,256]{3,2,1,0:T(8,128)(2,1)} convert(f32[2,19,16,256]{3,2,1,0:T(8,128)} %get-tuple-element.6) | non-fusion elementwise | flops 155648 | bytes 933888 | tf_op jit(solution)/shard_map/convert_element_type | solution.py:479
  39.5 0.0 copy-done
  39.5 102.2 %psum.7 = f32[2,20,128]{2,1,0:T(8,128)S(1)} all-reduce(f32[2,20,128]{2,1,0:T(8,128)S(1)} %copy-done), channel_id=1, replica_groups=mesh['gx'=128,'gy'=4] {'gx','gy'}, use_global_device_ids=true, to_apply=%region_0.0 | all-reduce | flops 5120 | bytes 40960 | tf_op jit(solution)/shard_map/psum | solution.py:477
  141.7 0.6 multiply_reduce_fusion.2
  143.0 0.5 divide_bitcast_fusion.2
  143.5 0.6 multiply_reduce_fusion
  145.5 0.6 divide_bitcast_fusion
Async XLA Ops:
  37.7 1.9 %copy-start = (f32[2,20,128]{2,1,0:T(8,128)S(1)}, f32[2,20,128]{2,1,0:T(8,128)}, u32[]{:S(2)}) copy-start(f32[2,20,128]{2,1,0:T(8,128)} %get-tuple-element.7) | copy-start | bytes 61444

commit v2 on v1

--- a/solution.py
+++ b/solution.py
@@ -46,6 +46,8 @@
 Y_MINUS = [(4, 0), (4, 1), (16, 0), (16, 1), (18, 0), (18, 1), (9, 0), (8, 1)]
 CORNERS = [7, 10, 8, 9]
 MESH = pl.DeviceIdType.MESH
+DEV_Z = 16
+PLANE = 32
 BF = jnp.bfloat16
 F32 = jnp.float32
 NT = (((1,), (1,)), ((), ()))
@@ -198,7 +200,7 @@
         dst[8 * k : 8 * k + 16, lanes] = two.astype(BF)
 
 
-def build_weights(w_in, b_in, w_out, w1, w1t, w2, w2t):
+def build_weights(w_in_t, b_in, w_out, w1, w1t, w2, w2t):
     comp_of = lax.broadcasted_iota(jnp.int32, (Q, DEPTH), 1) // 8
     expand = (lax.broadcasted_iota(jnp.int32, (Q, DEPTH), 0) == comp_of).astype(F32).astype(BF)
     comp_of_t = lax.broadcasted_iota(jnp.int32, (ROWS, Q), 0) // 8
@@ -216,10 +218,10 @@
         lax.broadcasted_iota(jnp.int32, (8, DEPTH), 1)
         == lax.broadcasted_iota(jnp.int32, (8, DEPTH), 0) + 8 * Q
     ).astype(F32).astype(BF)
-    in_rep = dot(w_in[...], expand)
+    in_rep = dot(w_in_t[...], expand, TN)
     bias_rep = dot(parts, place, TN)
     out_rep = dot(w_out[...], expand, TN)
-    in_rep_t = dot(expand_t, w_in[...], NT)
+    in_rep_t = dot(expand_t, w_in_t[...])
     out_rep_t = dot(expand_t, w_out[...])
     lane = lax.broadcasted_iota(jnp.int32, (UNITS, DEPTH), 1) % 8
     sub = lax.broadcasted_iota(jnp.int32, (ROWS, UNITS), 0) % 8
@@ -231,13 +233,102 @@
         w2[:, block] = jnp.where(sub == y, out_rep_t, 0.0).astype(BF)
 
 
-def kernel(pops, cot, flags, w_in, b_in, w_out, d0_ref, grads_ref, *scratch):
+class Reduction:
+    def __init__(self, refs, gx, gy):
+        (self.pay, self.rs_in, self.z_own, self.z_in, self.ag_own, self.ag, self.send,
+         self.recv) = refs
+        self.core = lax.rem(gx, 2)
+        self.z = lax.rem(gx // 2, DEV_Z)
+        self.y = gx // (2 * DEV_Z)
+        self.x = gy
+        self.me = (self.y * 4 + self.x) * 2 + self.core
+
+    def plane_peer(self, k):
+        m = lax.rem(self.me + k, PLANE)
+        return m, (((m // 8) * DEV_Z + self.z) * 2 + lax.rem(m, 2), lax.rem(m // 2, 4))
+
+    def line_peer(self, k):
+        z = lax.rem(self.z + k, DEV_Z)
+        return ((self.y * DEV_Z + z) * 2 + self.core, self.x)
+
+    def greet(self, barrier):
+        @pl.loop(1, PLANE)
+        def _(k):
+            pl.semaphore_signal(
+                barrier, inc=1, device_id=self.plane_peer(k)[1], device_id_type=MESH
+            )
+
+        @pl.loop(1, DEV_Z)
+        def _(k):
+            pl.semaphore_signal(barrier, inc=1, device_id=self.line_peer(k), device_id_type=MESH)
+
+        return PLANE + DEV_Z - 2
+
+    def remote(self, src, dst, phase, dev):
+        return pltpu.make_async_remote_copy(
+            src_ref=src, dst_ref=dst, send_sem=self.send.at[phase], recv_sem=self.recv.at[phase],
+            device_id=dev, device_id_type=MESH,
+        )
+
+    def wait(self, src, dst, phase):
+        dev = self.plane_peer(1)[1]
+        both = self.remote(src, dst, phase, dev)
+        both.wait_send()
+        both.wait_recv()
+
+    def scatter(self):
+        @pl.loop(1, PLANE)
+        def _(k):
+            m, dev = self.plane_peer(k)
+            self.remote(self.pay.at[m], self.rs_in.at[k - 1], 0, dev).start()
+
+    def finish(self):
+        self.wait(self.pay.at[0 : PLANE - 1], self.rs_in.at[:], 0)
+        part = self.pay[self.me] + jnp.sum(self.rs_in[...], axis=0)
+        self.z_own[...] = part
+        self.z_in[self.z] = part
+
+        @pl.loop(1, DEV_Z)
+        def _(k):
+            self.remote(self.z_own.at[:], self.z_in.at[self.z], 1, self.line_peer(k)).start()
+
+        sized = self.z_in.at[0 : DEV_Z - 1]
+        self.wait(sized, sized, 1)
+        total = jnp.sum(self.z_in[...], axis=0)
+        self.ag_own[...] = total
+        self.ag[self.me] = total
+
+        @pl.loop(1, PLANE)
+        def _(k):
+            dev = self.plane_peer(k)[1]
+            self.remote(self.ag_own.at[:], self.ag.at[self.me], 2, dev).start()
+
+        sized = self.ag.at[0 : PLANE - 1]
+        self.wait(sized, sized, 2)
+
+
+RED_SCRATCH = [
+    pltpu.VMEM((PLANE, 2, UNITS), F32),
+    pltpu.VMEM((PLANE - 1, 2, UNITS), F32),
+    pltpu.VMEM((2, UNITS), F32),
+    pltpu.VMEM((DEV_Z, 2, UNITS), F32),
+    pltpu.VMEM((2, UNITS), F32),
+    pltpu.VMEM((PLANE, 2, UNITS), F32),
+    pltpu.SemaphoreType.DMA((3,)),
+    pltpu.SemaphoreType.DMA((3,)),
+]
+N_RED = len(RED_SCRATCH)
+
+
+def kernel(pops, cot, flags, w_in_t, b_in, w_out, d0_ref, gin_ref, gb_ref, gout_ref, *scratch):
     gx, gy = lax.axis_index("gx"), lax.axis_index("gy")
+    reduction = Reduction(scratch[:N_RED], gx, gy)
+    scratch = scratch[N_RED:]
     ex_c = Exchange(scratch[:N_EX])
     ex_p = Exchange(scratch[N_EX : 2 * N_EX])
     ex_d = Exchange(scratch[2 * N_EX : 3 * N_EX])
     (w1, w1t, w2, w2t, feat0, feat1, qa, qb, hid0, hid1, ra, rb, t0, t1, gh, field, grad,
-     mom0, post) = scratch[3 * N_EX :]
+     mom0, post, out, out_sem) = scratch[3 * N_EX :]
 
     barrier = pltpu.get_barrier_semaphore()
     for dx in (1, 0, 127):
@@ -249,19 +340,17 @@
                 device_id=(lax.rem(gx + dx, 128), lax.rem(gy + dy, 4)), device_id_type=MESH,
             )
 
+    greeted = 8 + reduction.greet(barrier)
     for p in range(2):
         for i in range(Q):
             wide = cot[p, i].astype(F32)
             for s in range(2):
                 ex_c.put(OPPOSITE[i], p, s, wide[8 * s : 8 * s + 8, :])
-    build_weights(w_in, b_in, w_out, w1, w1t, w2, w2t)
+    build_weights(w_in_t, b_in, w_out, w1, w1t, w2, w2t)
     zero = jnp.zeros((DEPTH - ROWS, GROUPS * LANES), BF)
     for ref in (feat0, feat1, qa, qb):
         ref[ROWS:, :] = zero
-    pl.semaphore_wait(barrier, 8)
-    copies_c = ex_c.copies(gx, gy)
-    for c in copies_c:
-        c.start()
+    reduction.pay[...] = jnp.zeros((PLANE, 2, UNITS), F32)
 
     one = jnp.ones((8, LANES), F32)
     nil = jnp.zeros((8, LANES), F32)
@@ -306,6 +395,10 @@
 
     lax.fori_loop(0, GROUPS, step_a, 0)
 
+    pl.semaphore_wait(barrier, greeted)
+    copies_c = ex_c.copies(gx, gy)
+    for c in copies_c:
+        c.start()
     for g in range(GROUPS):
         for i in range(Q):
             ex_p.put(i, g // 2, g % 2, post[g, i])
@@ -340,13 +433,16 @@
         for i in range(Q):
             field[g, i] = ex_p.get(i, g // 2, g % 2)
 
-    def back(g, mom, act, r, put):
+    def preact_grad(g, act, r):
         lanes = lanes_of(g)
-        melt = melt_of(g)
         for c in range(4):
             block = pl.ds(256 * c, 256)
             t = act[block, lanes]
             r[block, lanes] = (gh[block, lanes] * (1.0 - t * t)).astype(BF)
+
+    def back(g, mom, r):
+        lanes = lanes_of(g)
+        melt = melt_of(g)
         prod = dot(w1t[...], r[:, lanes])
         m, wd = [], []
         for i in range(Q):
@@ -378,16 +474,13 @@
             val = (-0.25) * m[i] + INV_W[i] * prod[8 * i : 8 * i + 8, :] + drho
             if i:
                 val = val + along(i, dj)
-            put(i, val + (grad[g, o] - m[o]))
+            post[g, i] = val + (grad[g, o] - m[o])
 
     def step_b(g, carry):
         f = [field[g, i] for i in range(Q)]
         rho, mom, eq = front(f, g, feat1, hid1, t1)
-
-        def put(i, val):
-            post[g, i] = val
-
-        back(g, mom, t1, rb, put)
+        preact_grad(g, t1, rb)
+        back(g, mom, rb)
         return carry
 
     lax.fori_loop(0, GROUPS, step_b, 0)
@@ -407,18 +500,12 @@
         for i in range(Q):
             grad[g, i] = ex_d.get(OPPOSITE[i], g // 2, g % 2)
 
-    def step_c(g, carry):
+    def step_r(g, carry):
         hidden_grad(g, qa)
-        p = g // 2
-        rows = pl.ds(pl.multiple_of((g % 2) * 8, 8), 8)
-
-        def put(i, val):
-            d0_ref[p, i, rows, :] = val
-
-        back(g, [mom0[g, d] for d in range(3)], t0, ra, put)
+        preact_grad(g, t0, ra)
         return carry
 
-    lax.fori_loop(0, GROUPS, step_c, 0)
+    lax.fori_loop(0, GROUPS, step_r, 0)
     acc_out = acc_out + dot(qa[:ROWS, :], hid0[...], NT)
     acc_in = acc_in + dot(feat0[:ROWS, :], ra[...], NT)
     sub = lax.broadcasted_iota(jnp.int32, (ROWS, UNITS), 0) % 8
@@ -426,7 +513,33 @@
         tot = jnp.zeros((ROWS, UNITS), F32)
         for y in range(8):
             tot = tot + jnp.where(sub == y, acc[:, UNITS * y : UNITS * (y + 1)], 0.0)
-        grads_ref[k] = jnp.sum(tot.reshape(20, 8, UNITS), axis=1)
+        tot = jnp.sum(tot.reshape(20, 8, UNITS), axis=1)
+        for j in range(10):
+            reduction.pay[10 * k + j] = tot[2 * j : 2 * j + 2, :]
+    reduction.scatter()
+
+    def step_c(g, carry):
+        back(g, [mom0[g, d] for d in range(3)], ra)
+        return carry
+
+    lax.fori_loop(0, GROUPS, step_c, 0)
+    for p in range(2):
+        for i in range(Q):
+            out[p, i] = jnp.concatenate([post[2 * p, i], post[2 * p + 1, i]], axis=0).astype(BF)
+    write = pltpu.make_async_copy(out, d0_ref, out_sem)
+    write.start()
+    reduction.finish()
+
+    def normalized(rows):
+        total = jnp.concatenate(rows, axis=0)
+        scale = jnp.sum(total * total) / (total.shape[0] * UNITS) + 1e-06
+        return total / jnp.sqrt(scale)
+
+    row = [reduction.ag[k // 2, k % 2 : k % 2 + 1, :] for k in range(2 * 20)]
+    gin_ref[...] = normalized(row[:Q])
+    gb_ref[...] = normalized(row[Q : Q + 1])
+    gout_ref[...] = normalized(row[Q + 1 : 2 * Q + 1])
+    write.wait()
 
 
 def local_step(populations, cotangent, flags, w_in, b_in, w_out):
@@ -435,12 +548,15 @@
     return pl.pallas_call(
         kernel,
         out_shape=(
-            jax.ShapeDtypeStruct((2, Q, 16, LANES), F32),
-            jax.ShapeDtypeStruct((2, 20, UNITS), F32),
+            jax.ShapeDtypeStruct((2, Q, 16, LANES), BF),
+            jax.ShapeDtypeStruct((Q, UNITS), F32),
+            jax.ShapeDtypeStruct((1, UNITS), F32),
+            jax.ShapeDtypeStruct((Q, UNITS), F32),
         ),
         in_specs=[vmem] * 6,
-        out_specs=(vmem, vmem),
-        scratch_shapes=EX_SCRATCH * 3
+        out_specs=(pl.BlockSpec(memory_space=pl.ANY), vmem, vmem, vmem),
+        scratch_shapes=RED_SCRATCH
+        + EX_SCRATCH * 3
         + [
             pltpu.VMEM((HID, DEPTH), BF),
             pltpu.VMEM((ROWS, HID), BF),
@@ -461,26 +577,18 @@
             pltpu.VMEM((GROUPS, Q, 8, LANES), F32),
             pltpu.VMEM((GROUPS, 3, 8, LANES), F32),
             pltpu.VMEM((GROUPS, Q, 8, LANES), F32),
+            pltpu.VMEM((2, Q, 16, LANES), BF),
+            pltpu.SemaphoreType.DMA,
         ],
         compiler_params=pltpu.CompilerParams(
             collective_id=0, has_side_effects=True, vmem_limit_bytes=60 * 1024 * 1024
         ),
-    )(populations, cotangent, flags, w_in, b_in.reshape(1, UNITS), w_out)
-
-
-def normalized(total):
-    return total / jnp.sqrt(jnp.mean(total * total) + 1e-06)
+    )(populations, cotangent, flags, w_in.T, b_in.reshape(1, UNITS), w_out)
 
 
 def shards(populations, cotangent, flags, w_in, b_in, w_out):
-    d0, grads = local_step(populations, cotangent, flags, w_in, b_in, w_out)
-    totals = lax.psum(grads, ("gx", "gy"))
-    return (
-        d0.astype(BF),
-        normalized(totals[0, :Q].T),
-        normalized(totals[0, Q]),
-        normalized(totals[1, :Q]),
-    )
+    d0, grad_in, grad_b, grad_out = local_step(populations, cotangent, flags, w_in, b_in, w_out)
+    return d0, grad_in.T, grad_b.reshape(UNITS), grad_out
 
 
 def solution(mesh):

time: 146 us -> 58.4 us (0.40)
  blocking collectives: 102 us -> 0 us
  Pallas kernels: 35.6 us -> 54.1 us
  other arithmetic: 4.17 us -> 0 us
  between operations: 2.73 us -> 0.65 us
  local copies, waits for them, and re-layouts: 1.42 us -> 3.44 us
    psum x1 -> x0, blocking collectives: 102 us -> none  [shards(): totals = lax.psum(grads, ('gx', 'gy'))]
    pallas_call x1, Pallas kernels: 35.6 us -> 54.1 us  [local_step(): pl.pallas_call(kernel, out_shape=(jax.ShapeDtypeStruct((2, Q, 16, LANES),...]
    unnamed x3 -> x10, local copies, waits for them, and re-layouts: 1.42 us -> 3.44 us
    convert_element_type x1 -> x0, other arithmetic: 1.84 us -> none  [shards(): d0.astype(BF)]
where the time goes in v2:
time: 58.4 us; the launch traced here: 58.2 us
  Pallas kernels  54.1 us (93%)
  local copies, waits for them, and re-layouts  3.44 us (6%)
  between operations  0.65 us (1%)
    pallas_call x1, Pallas kernels, local_step(): pl.pallas_call(kernel, out_shape=(jax.ShapeDtypeStruct((2, Q, 16, LANES),...  54.1 us
    unnamed x10, local copies, waits for them, and re-layouts  3.44 us

profile of v2, /device:TPU:1, one launch (start us, length us, event | category | flops | bytes accessed | tf_op | source)
XLA Modules:
  0.0 58.2 jit_solution(14762364049515911118)
XLA Ops:
  0.6 54.1 %shard_map.93 = (bf16[2,19,16,256]{3,2,1,0:T(8,128)(2,1)}, f32[19,128]{1,0:T(8,128)}, f32[1,128]{1,0:T(1,128)}, f32[19,128]{1,0:T(8,128)}) custom-call(f32[2,19,16,256]{3,2,1,0:T(8,128)} %pops.1, bf16[2,19,16,256]{3,2,1,0:T(8,128)(2,1)} %cot.1, s32[2,16,256]{2,1,0:T(8,128)} %flags.1, bf16[19,128]{1,0:T(8,128)(2,1)} %bitcast.5, f32[1,128]{1,0:T(1,128)} %bitcast.6, ...), custom_call_target="tpu_custom_call" | custom-call | tf_op jit(solution)/shard_map/pallas_call | solution.py:548
  54.8 0.0 copy-start.1
  54.8 1.7 %copy.14 = bf16[2,19,16,256]{3,2,1,0:T(8,128)(2,1)} copy(bf16[2,19,16,256]{3,2,1,0:T(8,128)(2,1)} %get-tuple-element.16) | data formatting | bytes 622592
  56.5 0.0 copy-done.1
  56.5 0.0 copy-start.2
  56.5 0.0 copy-start
  56.5 0.6 %copy.15 = f32[128,19]{0,1:T(8,128)} copy(f32[128,19]{0,1:T(8,128)S(1)} %bitcast.4) | data formatting | bytes 19456
  57.1 0.0 copy-done.2
  57.1 0.5 copy.16
  57.6 0.0 copy-done
  57.6 0.6 %copy.17 = f32[19,128]{1,0:T(8,128)} copy(f32[19,128]{1,0:T(8,128)S(1)} %copy-done) | data formatting | bytes 19456
Async XLA Ops:
  54.8 1.7 %copy-start.1 = (f32[19,128]{1,0:T(8,128)S(1)}, f32[19,128]{1,0:T(8,128)}, u32[]{:S(2)}) copy-start(f32[19,128]{1,0:T(8,128)} %get-tuple-element.9) | copy-start | bytes 29188
  56.5 0.6 %copy-start.2 = (f32[1,128]{1,0:T(1,128)S(1)}, f32[1,128]{1,0:T(1,128)}, u32[]{:S(2)}) copy-start(f32[1,128]{1,0:T(1,128)} %get-tuple-element.10) | copy-start | bytes 1540
  56.5 1.1 %copy-start = (f32[19,128]{1,0:T(8,128)S(1)}, f32[19,128]{1,0:T(8,128)}, u32[]{:S(2)}) copy-start(f32[19,128]{1,0:T(8,128)} %get-tuple-element.19) | copy-start | bytes 29188

commit v3 on v2

v3 whole, which is shorter than its diff:
```python
import functools

import jax
import jax.numpy as jnp
from jax import lax
from jax.experimental import pallas as pl
from jax.experimental.pallas import tpu as pltpu
from jax.sharding import PartitionSpec as P

VELOCITY = [
    (0, 0, 0),
    (1, 0, 0),
    (-1, 0, 0),
    (0, 1, 0),
    (0, -1, 0),
    (0, 0, 1),
    (0, 0, -1),
    (1, 1, 0),
    (-1, -1, 0),
    (1, -1, 0),
    (-1, 1, 0),
    (1, 0, 1),
    (-1, 0, -1),
    (1, 0, -1),
    (-1, 0, 1),
    (0, 1, 1),
    (0, -1, -1),
    (0, 1, -1),
    (0, -1, 1),
]
OPPOSITE = [0, 2, 1, 4, 3, 6, 5, 8, 7, 10, 9, 12, 11, 14, 13, 16, 15, 18, 17]
INV_W = [3.0] + [18.0] * 6 + [36.0] * 12
W = [1.0 / 3.0] + [1.0 / 18.0] * 6 + [1.0 / 36.0] * 12
PAIRS = [(i, i + 1) for i in range(1, 19, 2)]
Q = 19
UNITS = 128
ROWS = 160
DEPTH = 256
HID = 8 * UNITS
LANES = 256
GROUPS = 4

X_PLUS = [1, 7, 9, 11, 13]
X_MINUS = [2, 8, 10, 12, 14]
Y_PLUS = [(3, 0), (3, 1), (15, 0), (15, 1), (17, 0), (17, 1), (7, 0), (10, 1)]
Y_MINUS = [(4, 0), (4, 1), (16, 0), (16, 1), (18, 0), (18, 1), (9, 0), (8, 1)]
CORNERS = [7, 10, 8, 9]
MESH = pl.DeviceIdType.MESH
DEV_Z = 16
PLANE = 32
CHUNK = 256
BF = jnp.bfloat16
F32 = jnp.float32
NT = (((1,), (1,)), ((), ()))
TN = (((0,), (0,)), ((), ()))


class Exchange:
    def __init__(self, refs):
        (self.own, self.sxp, self.sxm, self.syp, self.sym, self.rxl, self.rxr,
         self.ryl, self.ryu, self.rc, self.send, self.recv) = refs

    def put(self, j, p, s, val):
        cx, cy, cz = VELOCITY[j]
        if cz:
            val = pltpu.roll(val, cz % LANES, 1)
        rows = pl.ds(8 * s, 8)
        if cx == 1 and p == 1:
            self.sxp[X_PLUS.index(j), rows, :] = val
        elif cx == -1 and p == 0:
            self.sxm[X_MINUS.index(j), rows, :] = val
        else:
            self.own[p, j, rows, :] = val
        if cy == 1 and s == 1 and (j, p) in Y_PLUS:
            k = Y_PLUS.index((j, p))
            self.syp[k : k + 1, :] = val[7:8, :]
        if cy == -1 and s == 0 and (j, p) in Y_MINUS:
            k = Y_MINUS.index((j, p))
            self.sym[k : k + 1, :] = val[0:1, :]

    def send_half(self, s, near):
        rows = pl.ds(8 * s, 8)
        dy = 1 if s else -1
        plan = [
            (self.sxp.at[1 if s else 2, rows, :], self.rc.at[0 if s else 3], near(1, dy)),
            (self.sxm.at[2 if s else 1, rows, :], self.rc.at[1 if s else 2], near(-1, dy)),
            (self.sxp.at[:, rows, :], self.rxl.at[:, rows, :], near(1, 0)),
            (self.sxm.at[:, rows, :], self.rxr.at[:, rows, :], near(-1, 0)),
            (self.syp, self.ryl, near(0, 1)) if s else (self.sym, self.ryu, near(0, -1)),
        ]
        made = [
            pltpu.make_async_remote_copy(
                src_ref=src, dst_ref=dst, send_sem=self.send.at[5 * s + k],
                recv_sem=self.recv.at[5 * s + k], device_id=dev, device_id_type=MESH,
            )
            for k, (src, dst, dev) in enumerate(plan)
        ]
        for c in made:
            c.start()
        return made

    def get(self, j, p, s):
        cx, cy, cz = VELOCITY[j]
        q = p - cx
        if q == -1:
            src = self.rxl.at[X_PLUS.index(j)]
        elif q == 2:
            src = self.rxr.at[X_MINUS.index(j)]
        else:
            src = self.own.at[q, j]
        if cy == 0:
            return src[8 * s : 8 * s + 8, :]
        row = lax.broadcasted_iota(jnp.int32, (8, LANES), 0)
        if cy == 1:
            if s == 1:
                return src[7:15, :]
            if q in (0, 1):
                k = Y_PLUS.index((j, q))
                halo = self.ryl[k : k + 1, :]
            else:
                halo = self.rc[CORNERS.index(j), 7:8, :]
            return jnp.where(row == 0, halo, pltpu.roll(src[0:8, :], 1, 0))
        if s == 0:
            return src[1:9, :]
        if q in (0, 1):
            k = Y_MINUS.index((j, q))
            halo = self.ryu[k : k + 1, :]
        else:
            halo = self.rc[CORNERS.index(j), 0:1, :]
        return jnp.where(row == 7, halo, pltpu.roll(src[8:16, :], 7, 0))


EX_SCRATCH = [
    pltpu.VMEM((2, Q, 16, LANES), F32),
    pltpu.VMEM((5, 16, LANES), F32),
    pltpu.VMEM((5, 16, LANES), F32),
    pltpu.VMEM((8, LANES), F32),
    pltpu.VMEM((8, LANES), F32),
    pltpu.VMEM((5, 16, LANES), F32),
    pltpu.VMEM((5, 16, LANES), F32),
    pltpu.VMEM((8, LANES), F32),
    pltpu.VMEM((8, LANES), F32),
    pltpu.VMEM((4, 8, LANES), F32),
    pltpu.SemaphoreType.DMA((10,)),
    pltpu.SemaphoreType.DMA((10,)),
]
N_EX = len(EX_SCRATCH)


def dot(a, b, dims=None):
    if dims is None:
        return jnp.dot(a, b, preferred_element_type=F32)
    return lax.dot_general(a, b, dims, preferred_element_type=F32)


def moments(f):
    rho = f[0]
    for a, b in PAIRS:
        rho = rho + (f[a] + f[b])
    mom = []
    for d in range(3):
        acc = None
        for a, b in PAIRS:
            c = VELOCITY[a][d]
            if c == 0:
                continue
            diff = f[a] - f[b] if c == 1 else f[b] - f[a]
            acc = diff if acc is None else acc + diff
        mom.append(acc)
    return rho, mom


def along(i, vec):
    out = None
    for d in range(3):
        c = VELOCITY[i][d]
        if c == 0:
            continue
        if out is None:
            out = vec[d] if c == 1 else -vec[d]
        else:
            out = out + vec[d] if c == 1 else out - vec[d]
    return out


def equilibrium(rho, mom):
    base = rho - 1.5 * (mom[0] * mom[0] + mom[1] * mom[1] + mom[2] * mom[2])
    eq = [base]
    for a, b in PAIRS:
        u = along(a, mom)
        even = base + 4.5 * (u * u)
        odd = 3.0 * u
        eq.append(even + odd)
        eq.append(even - odd)
    return eq


def store_features(dst, lanes, vals):
    for k in range(0, len(vals), 2):
        two = jnp.concatenate([vals[k], vals[k + 1]], axis=0)
        dst[8 * k : 8 * k + 16, lanes] = two.astype(BF)


def one_hot(hit):
    return hit.astype(F32).astype(BF)


def iota(shape, dim):
    return lax.broadcasted_iota(jnp.int32, shape, dim)


def tall(w_t, masked, extra=None):
    expand = one_hot(iota((Q, DEPTH), 0) == iota((Q, DEPTH), 1) // 8)
    wide = dot(w_t, expand, TN)
    lane = iota((UNITS, DEPTH), 1) % 8
    for y in range(8):
        val = jnp.where(lane == y, wide, 0.0)
        if extra is not None:
            val = val + extra
        masked[pl.ds(UNITS * y, UNITS), :] = val.astype(BF)


def flat(w_t, masked):
    expand = one_hot(iota((ROWS, Q), 1) == iota((ROWS, Q), 0) // 8)
    wide = dot(expand, w_t)
    sub = iota((ROWS, UNITS), 0) % 8
    for y in range(8):
        masked[:, pl.ds(UNITS * y, UNITS)] = jnp.where(sub == y, wide, 0.0).astype(BF)


def bias_columns(b_in):
    hi = b_in.astype(BF)
    rest = b_in - hi.astype(F32)
    mid = rest.astype(BF)
    low = (rest - mid.astype(F32)).astype(BF)
    row = iota((8, UNITS), 0)
    parts = jnp.where(
        row == 0, hi.astype(F32),
        jnp.where(row == 1, mid.astype(F32), jnp.where(row == 2, low.astype(F32), 0.0)),
    ).astype(BF)
    place = one_hot(iota((8, DEPTH), 1) == iota((8, DEPTH), 0) + 8 * Q)
    return dot(parts, place, TN)


class Reduction:
    def __init__(self, refs, gx, gy):
        (self.pay, self.rs_in, self.z_own, self.z_in, self.ag_own, self.ag, self.send,
         self.recv) = refs
        self.z = lax.rem(gx // 2, DEV_Z)
        core, y = lax.rem(gx, 2), gx // (2 * DEV_Z)
        self.me = y * 8 + gy * 2 + core
        cs = [core, 1 - core]
        xs = [gy] + [lax.rem(gy + k, 4) for k in range(1, 4)]
        ys = [y] + [lax.rem(y + k, 4) for k in range(1, 4)]
        self.plane = []
        for dy in range(4):
            base, mbase = ys[dy] * (2 * DEV_Z) + self.z * 2, ys[dy] * 8
            for dc in range(2):
                for dx in range(4):
                    if dx or dy or dc:
                        dev = (base + cs[dc], xs[dx])
                        self.plane.append((mbase + (xs[dx] * 2 + cs[dc]), dev))
        line = gx - 2 * self.z
        self.line = []
        for k in range(1, DEV_Z):
            self.line.append((line + 2 * lax.rem(self.z + k, DEV_Z), gy))

    def greet(self, barrier):
        for dev in [d for _, d in self.plane] + self.line:
            pl.semaphore_signal(barrier, inc=1, device_id=dev, device_id_type=MESH)
        return PLANE + DEV_Z - 2

    def remote(self, src, dst, phase, dev):
        return pltpu.make_async_remote_copy(
            src_ref=src, dst_ref=dst, send_sem=self.send.at[phase], recv_sem=self.recv.at[phase],
            device_id=dev, device_id_type=MESH,
        )

    def wait(self, src, dst, phase):
        dev = self.plane[0][1]
        both = self.remote(src, dst, phase, dev)
        both.wait_send()
        both.wait_recv()

    def scatter(self):
        for k, (m, dev) in enumerate(self.plane):
            self.remote(self.pay.at[m], self.rs_in.at[k], 0, dev).start()

    def finish(self):
        self.wait(self.pay.at[0 : PLANE - 1], self.rs_in.at[:], 0)
        part = self.pay[self.me] + jnp.sum(self.rs_in[...], axis=0)
        self.z_own[...] = part
        self.z_in[self.z] = part

        for dev in self.line:
            self.remote(self.z_own.at[:], self.z_in.at[self.z], 1, dev).start()

        sized = self.z_in.at[0 : DEV_Z - 1]
        self.wait(sized, sized, 1)
        total = jnp.sum(self.z_in[...], axis=0)
        self.ag_own[...] = total
        self.ag[self.me] = total

        for _, dev in self.plane:
            self.remote(self.ag_own.at[:], self.ag.at[self.me], 2, dev).start()

        sized = self.ag.at[0 : PLANE - 1]
        self.wait(sized, sized, 2)


RED_SCRATCH = [
    pltpu.VMEM((PLANE, 2, UNITS), F32),
    pltpu.VMEM((PLANE - 1, 2, UNITS), F32),
    pltpu.VMEM((2, UNITS), F32),
    pltpu.VMEM((DEV_Z, 2, UNITS), F32),
    pltpu.VMEM((2, UNITS), F32),
    pltpu.VMEM((PLANE, 2, UNITS), F32),
    pltpu.SemaphoreType.DMA((3,)),
    pltpu.SemaphoreType.DMA((3,)),
]
N_RED = len(RED_SCRATCH)


def kernel(pops_hbm, cot_hbm, flags, w_in_t, b_in, w_out, d0_ref, gin_ref, gb_ref, gout_ref, *scratch):
    gx, gy = lax.axis_index("gx"), lax.axis_index("gy")
    (w1, w1t, w2, w2t, feat0, feat1, qa, qb, hid0, hid1, ra, rb, t0, t1, gh, field, grad,
     mom0, post, out, fold_out, pops, cot, out_sem, in_sem) = scratch[N_RED + 3 * N_EX :]
    get_cot = pltpu.make_async_copy(cot_hbm, cot, in_sem.at[0])
    get_pops = pltpu.make_async_copy(pops_hbm, pops, in_sem.at[1])
    get_cot.start()
    get_pops.start()
    reduction = Reduction(scratch[:N_RED], gx, gy)
    ex_c, ex_p, ex_d = [
        Exchange(scratch[N_RED + k * N_EX : N_RED + (k + 1) * N_EX]) for k in range(3)
    ]
    step_x = {0: gx, 1: lax.rem(gx + 1, 128), -1: lax.rem(gx + 127, 128)}
    step_y = {0: gy, 1: lax.rem(gy + 1, 4), -1: lax.rem(gy + 3, 4)}

    def near(dx, dy):
        return (step_x[dx], step_y[dy])

    barrier = pltpu.get_barrier_semaphore()
    for dx in (1, 0, -1):
        for dy in (1, 0, -1):
            if dx or dy:
                pl.semaphore_signal(
                    barrier, inc=1, device_id=near(dx, dy), device_id_type=MESH
                )
    greeted = 8 + reduction.greet(barrier)
    tall(w_in_t[...], w1, bias_columns(b_in[...]))
    flat(w_out[...], w2)
    zero = jnp.zeros((DEPTH - ROWS, GROUPS * LANES), BF)
    for ref in (feat0, feat1, qa, qb):
        ref[ROWS:, :] = zero
    reduction.pay[...] = jnp.zeros((PLANE, 2, UNITS), F32)
    get_cot.wait()
    for p in range(2):
        for i in range(Q):
            wide = cot[p, i].astype(F32)
            for s in range(2):
                ex_c.put(OPPOSITE[i], p, s, wide[8 * s : 8 * s + 8, :])
    one = jnp.ones((8, LANES), F32)
    nil = jnp.zeros((8, LANES), F32)
    get_pops.wait()

    def lanes_of(p, s):
        return pl.ds((2 * p + s) * LANES, LANES)

    def rows_of(s):
        return pl.ds(8 * s, 8)

    def melt_of(p, s):
        return flags[p, rows_of(s), :].astype(F32)

    def front(f, p, s, feat, hid, act):
        rho, mom = moments(f)
        eq = equilibrium(rho, mom)
        lanes = lanes_of(p, s)
        store_features(feat, lanes, [f[i] * INV_W[i] - eq[i] for i in range(Q)] + [one])
        for c in range(0, HID, CHUNK):
            block = pl.ds(c, CHUNK)
            t = jnp.tanh(dot(w1[block, :], feat[:, lanes]))
            act[block, lanes] = t
            hid[block, lanes] = t.astype(BF)
        return rho, mom, eq

    def step_a(p, s):
        f = [pops[p, i, rows_of(s), :] for i in range(Q)]
        rho, mom, eq = front(f, p, s, feat0, hid0, t0)
        for d in range(3):
            mom0[2 * p + s, d] = mom[d]
        learned = dot(w2[...], hid0[:, lanes_of(p, s)])
        melt = melt_of(p, s) > 0.5
        excess = rho - 1.0
        for i in range(Q):
            val = -0.25 * f[i] + (1.25 * W[i]) * eq[i] + learned[8 * i : 8 * i + 8, :]
            cz = VELOCITY[i][2]
            if cz:
                val = val + (0.15 * W[i] * cz) * excess
            ex_p.put(i, p, s, jnp.where(melt, val, f[OPPOSITE[i]]))

    copies_c, copies_p, copies_d = [], [], []
    for p in range(2):
        step_a(p, 1)
    pl.semaphore_wait(barrier, greeted)
    copies_c += ex_c.send_half(1, near)
    copies_c += ex_c.send_half(0, near)
    copies_p += ex_p.send_half(1, near)
    for p in range(2):
        step_a(p, 0)
    copies_p += ex_p.send_half(0, near)

    tall(w_out[...], w2t)
    flat(w_in_t[...], w1t)
    for c in copies_c:
        c.wait()

    def hidden_grad(p, s, q):
        melt = melt_of(p, s)
        m = [grad[2 * p + s, i] * melt for i in range(Q)]
        store_features(q, lanes_of(p, s), m + [nil])

    for p in range(2):
        for s in range(2):
            for i in range(Q):
                grad[2 * p + s, i] = ex_c.get(OPPOSITE[i], p, s)
            hidden_grad(p, s, qb)
            for c in range(0, HID, CHUNK):
                block = pl.ds(c, CHUNK)
                gh[block, lanes_of(p, s)] = dot(w2t[block, :], qb[:, lanes_of(p, s)])

    for c in copies_p:
        c.wait()

    def back(p, s, mom, r, put):
        g = 2 * p + s
        melt = melt_of(p, s)
        prod = dot(w1t[...], r[:, lanes_of(p, s)])
        m, wd = [], []
        for i in range(Q):
            m.append(grad[g, i] * melt)
            wd.append((1.25 * W[i]) * m[i] - prod[8 * i : 8 * i + 8, :])
        total = wd[0]
        lift = None
        dj = [None, None, None]
        for a, b in PAIRS:
            both = wd[a] + wd[b]
            total = total + both
            cz = VELOCITY[a][2]
            if cz:
                term = (0.15 * W[a] * cz) * (m[a] - m[b])
                lift = term if lift is None else lift + term
            slope = 3.0 * (wd[a] - wd[b]) + 9.0 * along(a, mom) * both
            for d in range(3):
                c = VELOCITY[a][d]
                if c == 0:
                    continue
                if dj[d] is None:
                    dj[d] = slope if c == 1 else -slope
                else:
                    dj[d] = dj[d] + slope if c == 1 else dj[d] - slope
        drho = total + lift
        dj = [dj[d] - 3.0 * mom[d] * total for d in range(3)]
        for i in range(Q):
            o = OPPOSITE[i]
            val = (-0.25) * m[i] + INV_W[i] * prod[8 * i : 8 * i + 8, :] + drho
            if i:
                val = val + along(i, dj)
            put(i, val + (grad[g, o] - m[o]))

    def step_b(p, s):
        f = [ex_p.get(i, p, s) for i in range(Q)]
        _, mom, _ = front(f, p, s, feat1, hid1, t1)
        lanes = lanes_of(p, s)
        for c in range(0, HID, CHUNK):
            block = pl.ds(c, CHUNK)
            t = t1[block, lanes]
            rb[block, lanes] = (gh[block, lanes] * (1.0 - t * t)).astype(BF)
        back(p, s, mom, rb, lambda i, val: ex_d.put(OPPOSITE[i], p, s, val))

    for s in (1, 0):
        for p in range(2):
            step_b(p, s)
        copies_d += ex_d.send_half(s, near)

    def weight_sums(feat, r, q, hid):
        sub = iota((ROWS, UNITS), 0) % 8
        sums = []
        for left, right in ((feat, r), (q, hid)):
            tot = None
            for c in range(0, HID, 256):
                acc = dot(left[:ROWS, :], right[pl.ds(c, 256), :], NT)
                for k in range(2):
                    hit = jnp.where(sub == c // UNITS + k, acc[:, UNITS * k : UNITS * (k + 1)], 0.0)
                    tot = hit if tot is None else tot + hit
            sums.append(jnp.sum(tot.reshape(20, 8, UNITS), axis=1))
        return sums

    for k, val in enumerate(weight_sums(feat1, rb, qb, hid1)):
        fold_out[0, k] = val
    for c in range(0, HID, CHUNK):
        block = pl.ds(c, CHUNK)
        t = t0[block, :]
        t0[block, :] = 1.0 - t * t

    for c in copies_d:
        c.wait()
    for p in range(2):
        for s in range(2):
            for i in range(Q):
                grad[2 * p + s, i] = ex_d.get(OPPOSITE[i], p, s)
            hidden_grad(p, s, qa)
            lanes = lanes_of(p, s)
            for c in range(0, HID, CHUNK):
                block = pl.ds(c, CHUNK)
                ra[block, lanes] = (dot(w2t[block, :], qa[:, lanes]) * t0[block, lanes]).astype(BF)

    for k, val in enumerate(weight_sums(feat0, ra, qa, hid0)):
        tot = val + fold_out[0, k]
        for j in range(10):
            reduction.pay[10 * k + j] = tot[2 * j : 2 * j + 2, :]
    reduction.scatter()

    def keep(p, s):
        def put(i, val):
            post[2 * p + s, i] = val

        return put

    for p in range(2):
        for s in range(2):
            back(p, s, [mom0[2 * p + s, d] for d in range(3)], ra, keep(p, s))
        for i in range(Q):
            out[p, i] = jnp.concatenate([post[2 * p, i], post[2 * p + 1, i]], axis=0).astype(BF)
    write = pltpu.make_async_copy(out, d0_ref, out_sem)
    write.start()
    reduction.finish()

    def normalized(rows):
        total = jnp.concatenate(rows, axis=0)
        scale = jnp.sum(total * total) / (total.shape[0] * UNITS) + 1e-06
        return total / jnp.sqrt(scale)

    row = [reduction.ag[k // 2, k % 2 : k % 2 + 1, :] for k in range(2 * 20)]
    gin_ref[...] = normalized(row[:Q])
    gb_ref[...] = normalized(row[Q : Q + 1])
    gout_ref[...] = normalized(row[Q + 1 : 2 * Q + 1])
    write.wait()


def local_step(populations, cotangent, flags, w_in, b_in, w_out):
    vmem = pl.BlockSpec(memory_space=pltpu.VMEM)
    hbm = pl.BlockSpec(memory_space=pl.ANY)
    cells = GROUPS * LANES
    return pl.pallas_call(
        kernel,
        out_shape=(
            jax.ShapeDtypeStruct((2, Q, 16, LANES), BF),
            jax.ShapeDtypeStruct((Q, UNITS), F32),
            jax.ShapeDtypeStruct((1, UNITS), F32),
            jax.ShapeDtypeStruct((Q, UNITS), F32),
        ),
        in_specs=[hbm] * 2 + [vmem] * 4,
        out_specs=(pl.BlockSpec(memory_space=pl.ANY), vmem, vmem, vmem),
        scratch_shapes=RED_SCRATCH
        + EX_SCRATCH * 3
        + [
            pltpu.VMEM((HID, DEPTH), BF),
            pltpu.VMEM((ROWS, HID), BF),
            pltpu.VMEM((ROWS, HID), BF),
            pltpu.VMEM((HID, DEPTH), BF),
            pltpu.VMEM((DEPTH, cells), BF),
            pltpu.VMEM((DEPTH, cells), BF),
            pltpu.VMEM((DEPTH, cells), BF),
            pltpu.VMEM((DEPTH, cells), BF),
            pltpu.VMEM((HID, cells), BF),
            pltpu.VMEM((HID, cells), BF),
            pltpu.VMEM((HID, cells), BF),
            pltpu.VMEM((HID, cells), BF),
            pltpu.VMEM((HID, cells), F32),
            pltpu.VMEM((HID, cells), F32),
            pltpu.VMEM((HID, cells), F32),
            pltpu.VMEM((GROUPS, Q, 8, LANES), F32),
            pltpu.VMEM((GROUPS, Q, 8, LANES), F32),
            pltpu.VMEM((GROUPS, 3, 8, LANES), F32),
            pltpu.VMEM((GROUPS, Q, 8, LANES), F32),
            pltpu.VMEM((2, Q, 16, LANES), BF),
            pltpu.VMEM((2, 2, 20, UNITS), F32),
            pltpu.VMEM((2, Q, 16, LANES), F32),
            pltpu.VMEM((2, Q, 16, LANES), BF),
            pltpu.SemaphoreType.DMA,
            pltpu.SemaphoreType.DMA((2,)),
        ],
        compiler_params=pltpu.CompilerParams(
            collective_id=0, has_side_effects=True, vmem_limit_bytes=60 * 1024 * 1024
        ),
    )(populations, cotangent, flags, w_in.T, b_in.reshape(1, UNITS), w_out)


def shards(populations, cotangent, flags, w_in, b_in, w_out):
    d0, grad_in, grad_b, grad_out = local_step(populations, cotangent, flags, w_in, b_in, w_out)
    return d0, grad_in.T, grad_b.reshape(UNITS), grad_out


def solution(mesh):
    placed = (
        P("gx", None, "gy", None),
        P("gx", None, "gy", None),
        P("gx", "gy", None),
        P(),
        P(),
        P(),
    )
    return jax.shard_map(
        shards,
        mesh=mesh,
        in_specs=placed,
        out_specs=(P("gx", None, "gy", None), P(), P(), P()),
        check_vma=False,
    )
```

time: 58.4 us -> 52.5 us (0.90)
  Pallas kernels: 54.1 us -> 48.2 us
    pallas_call x1, Pallas kernels: 54.1 us -> 48.2 us  [local_step(): pl.pallas_call(kernel, out_shape=(jax.ShapeDtypeStruct((2, Q, 16, LANES),...]
where the time goes in v3:
time: 52.5 us; the launch traced here: 52.3 us
  Pallas kernels  48.2 us (92%)
  local copies, waits for them, and re-layouts  3.44 us (7%)
  between operations  0.65 us (1%)
    pallas_call x1, Pallas kernels, local_step(): pl.pallas_call(kernel, out_shape=(jax.ShapeDtypeStruct((2, Q, 16, LANES),...  48.2 us
    unnamed x10, local copies, waits for them, and re-layouts  3.44 us

profile of v3, /device:TPU:1, one launch (start us, length us, event | category | flops | bytes accessed | tf_op | source)
XLA Modules:
  0.0 52.3 jit_solution(4507943520379941855)
XLA Ops:
  0.6 48.2 %shard_map.93 = (bf16[2,19,16,256]{3,2,1,0:T(8,128)(2,1)}, f32[19,128]{1,0:T(8,128)}, f32[1,128]{1,0:T(1,128)}, f32[19,128]{1,0:T(8,128)}) custom-call(f32[2,19,16,256]{3,2,1,0:T(8,128)} %pops_hbm.1, bf16[2,19,16,256]{3,2,1,0:T(8,128)(2,1)} %cot_hbm.1, s32[2,16,256]{2,1,0:T(8,128)} %flags.1, bf16[19,128]{1,0:T(8,128)(2,1)} %bitcast.5, f32[1,128]{1,0:T(1,128)} %bitcast.6, ...), custom_call_target="tpu_custom_call" | custom-call | tf_op jit(solution)/shard_map/pallas_call | solution.py:555
  48.8 0.0 copy-start.1
  48.8 1.7 %copy.14 = bf16[2,19,16,256]{3,2,1,0:T(8,128)(2,1)} copy(bf16[2,19,16,256]{3,2,1,0:T(8,128)(2,1)} %get-tuple-element.16) | data formatting | bytes 622592
  50.5 0.0 copy-done.1
  50.5 0.0 copy-start.2
  50.6 0.0 copy-start
  50.6 0.6 %copy.15 = f32[128,19]{0,1:T(8,128)} copy(f32[128,19]{0,1:T(8,128)S(1)} %bitcast.4) | data formatting | bytes 19456
  51.2 0.0 copy-done.2
  51.2 0.5 copy.16
  51.7 0.0 copy-done
  51.7 0.6 %copy.17 = f32[19,128]{1,0:T(8,128)} copy(f32[19,128]{1,0:T(8,128)S(1)} %copy-done) | data formatting | bytes 19456
Async XLA Ops:
  48.8 1.7 %copy-start.1 = (f32[19,128]{1,0:T(8,128)S(1)}, f32[19,128]{1,0:T(8,128)}, u32[]{:S(2)}) copy-start(f32[19,128]{1,0:T(8,128)} %get-tuple-element.9) | copy-start | bytes 29188
  50.5 0.6 %copy-start.2 = (f32[1,128]{1,0:T(1,128)S(1)}, f32[1,128]{1,0:T(1,128)}, u32[]{:S(2)}) copy-start(f32[1,128]{1,0:T(1,128)} %get-tuple-element.10) | copy-start | bytes 1540
  50.6 1.1 %copy-start = (f32[19,128]{1,0:T(8,128)S(1)}, f32[19,128]{1,0:T(8,128)}, u32[]{:S(2)}) copy-start(f32[19,128]{1,0:T(8,128)} %get-tuple-element.19) | copy-start | bytes 29188

commit v4 on v3

--- a/solution.py
+++ b/solution.py
@@ -243,9 +243,9 @@
 
 
 class Reduction:
-    def __init__(self, refs, gx, gy):
-        (self.pay, self.rs_in, self.z_own, self.z_in, self.ag_own, self.ag, self.send,
-         self.recv) = refs
+    def __init__(self, refs, ag, gx, gy):
+        (self.pay, self.rs_in, self.z_own, self.z_in, self.ag_own, self.send, self.recv) = refs
+        self.ag = ag
         self.z = lax.rem(gx // 2, DEV_Z)
         core, y = lax.rem(gx, 2), gx // (2 * DEV_Z)
         self.me = y * 8 + gy * 2 + core
@@ -314,22 +314,26 @@
     pltpu.VMEM((2, UNITS), F32),
     pltpu.VMEM((DEV_Z, 2, UNITS), F32),
     pltpu.VMEM((2, UNITS), F32),
-    pltpu.VMEM((PLANE, 2, UNITS), F32),
     pltpu.SemaphoreType.DMA((3,)),
     pltpu.SemaphoreType.DMA((3,)),
 ]
 N_RED = len(RED_SCRATCH)
 
 
-def kernel(pops_hbm, cot_hbm, flags, w_in_t, b_in, w_out, d0_ref, gin_ref, gb_ref, gout_ref, *scratch):
+def kernel(pops_hbm, cot_hbm, *refs):
+    small_hbm, (out, ag), scratch = refs[:4], refs[4:6], refs[6:]
     gx, gy = lax.axis_index("gx"), lax.axis_index("gy")
     (w1, w1t, w2, w2t, feat0, feat1, qa, qb, hid0, hid1, ra, rb, t0, t1, gh, field, grad,
-     mom0, post, out, fold_out, pops, cot, out_sem, in_sem) = scratch[N_RED + 3 * N_EX :]
+     mom0, post, fold_out, pops, cot, flags, w_in_t, b_in, w_out, in_sem) = scratch[N_RED + 3 * N_EX :]
     get_cot = pltpu.make_async_copy(cot_hbm, cot, in_sem.at[0])
     get_pops = pltpu.make_async_copy(pops_hbm, pops, in_sem.at[1])
-    get_cot.start()
-    get_pops.start()
-    reduction = Reduction(scratch[:N_RED], gx, gy)
+    gets = [
+        pltpu.make_async_copy(src, dst, in_sem.at[2 + k])
+        for k, (src, dst) in enumerate(zip(small_hbm, (flags, w_in_t, b_in, w_out)))
+    ]
+    for c in gets[1:] + [get_cot, get_pops, gets[0]]:
+        c.start()
+    reduction = Reduction(scratch[:N_RED], ag, gx, gy)
     ex_c, ex_p, ex_d = [
         Exchange(scratch[N_RED + k * N_EX : N_RED + (k + 1) * N_EX]) for k in range(3)
     ]
@@ -347,6 +351,8 @@
                     barrier, inc=1, device_id=near(dx, dy), device_id_type=MESH
                 )
     greeted = 8 + reduction.greet(barrier)
+    for c in gets[1:]:
+        c.wait()
     tall(w_in_t[...], w1, bias_columns(b_in[...]))
     flat(w_out[...], w2)
     zero = jnp.zeros((DEPTH - ROWS, GROUPS * LANES), BF)
@@ -362,6 +368,7 @@
     one = jnp.ones((8, LANES), F32)
     nil = jnp.zeros((8, LANES), F32)
     get_pops.wait()
+    gets[0].wait()
 
     def lanes_of(p, s):
         return pl.ds((2 * p + s) * LANES, LANES)
@@ -532,16 +539,19 @@
             back(p, s, [mom0[2 * p + s, d] for d in range(3)], ra, keep(p, s))
         for i in range(Q):
             out[p, i] = jnp.concatenate([post[2 * p, i], post[2 * p + 1, i]], axis=0).astype(BF)
-    write = pltpu.make_async_copy(out, d0_ref, out_sem)
+    reduction.finish()
+
+
+def finish_kernel(d0, ag, d0_ref, gin_ref, gb_ref, gout_ref, sem):
+    write = pltpu.make_async_copy(d0, d0_ref, sem)
     write.start()
-    reduction.finish()
 
     def normalized(rows):
         total = jnp.concatenate(rows, axis=0)
         scale = jnp.sum(total * total) / (total.shape[0] * UNITS) + 1e-06
         return total / jnp.sqrt(scale)
 
-    row = [reduction.ag[k // 2, k % 2 : k % 2 + 1, :] for k in range(2 * 20)]
+    row = [ag[k // 2, k % 2 : k % 2 + 1, :] for k in range(2 * 20)]
     gin_ref[...] = normalized(row[:Q])
     gb_ref[...] = normalized(row[Q : Q + 1])
     gout_ref[...] = normalized(row[Q + 1 : 2 * Q + 1])
@@ -550,18 +560,16 @@
 
 def local_step(populations, cotangent, flags, w_in, b_in, w_out):
     vmem = pl.BlockSpec(memory_space=pltpu.VMEM)
-    hbm = pl.BlockSpec(memory_space=pl.ANY)
+    hbm = pl.BlockSpec(memory_space=pltpu.HBM)
     cells = GROUPS * LANES
-    return pl.pallas_call(
+    d0, ag = pl.pallas_call(
         kernel,
         out_shape=(
-            jax.ShapeDtypeStruct((2, Q, 16, LANES), BF),
-            jax.ShapeDtypeStruct((Q, UNITS), F32),
-            jax.ShapeDtypeStruct((1, UNITS), F32),
-            jax.ShapeDtypeStruct((Q, UNITS), F32),
+            pltpu.VMEM((2, Q, 16, LANES), BF),
+            pltpu.VMEM((PLANE, 2, UNITS), F32),
         ),
-        in_specs=[hbm] * 2 + [vmem] * 4,
-        out_specs=(pl.BlockSpec(memory_space=pl.ANY), vmem, vmem, vmem),
+        in_specs=[hbm] * 6,
+        out_specs=(vmem, vmem),
         scratch_shapes=RED_SCRATCH
         + EX_SCRATCH * 3
         + [
@@ -584,17 +592,32 @@
             pltpu.VMEM((GROUPS, Q, 8, LANES), F32),
             pltpu.VMEM((GROUPS, 3, 8, LANES), F32),
             pltpu.VMEM((GROUPS, Q, 8, LANES), F32),
-            pltpu.VMEM((2, Q, 16, LANES), BF),
             pltpu.VMEM((2, 2, 20, UNITS), F32),
             pltpu.VMEM((2, Q, 16, LANES), F32),
             pltpu.VMEM((2, Q, 16, LANES), BF),
-            pltpu.SemaphoreType.DMA,
-            pltpu.SemaphoreType.DMA((2,)),
+            pltpu.VMEM((2, 16, LANES), jnp.int32),
+            pltpu.VMEM((Q, UNITS), BF),
+            pltpu.VMEM((1, UNITS), F32),
+            pltpu.VMEM((Q, UNITS), BF),
+            pltpu.SemaphoreType.DMA((6,)),
         ],
         compiler_params=pltpu.CompilerParams(
-            collective_id=0, has_side_effects=True, vmem_limit_bytes=60 * 1024 * 1024
+            collective_id=0, has_side_effects=True, vmem_limit_bytes=66650112
         ),
     )(populations, cotangent, flags, w_in.T, b_in.reshape(1, UNITS), w_out)
+    return pl.pallas_call(
+        finish_kernel,
+        out_shape=(
+            jax.ShapeDtypeStruct((2, Q, 16, LANES), BF),
+            jax.ShapeDtypeStruct((Q, UNITS), F32),
+            jax.ShapeDtypeStruct((1, UNITS), F32),
+            jax.ShapeDtypeStruct((Q, UNITS), F32),
+        ),
+        in_specs=[vmem] * 2,
+        out_specs=(hbm, vmem, vmem, vmem),
+        scratch_shapes=[pltpu.SemaphoreType.DMA],
+        compiler_params=pltpu.CompilerParams(vmem_limit_bytes=1024 * 1024),
+    )(d0, ag)
 
 
 def shards(populations, cotangent, flags, w_in, b_in, w_out):

time: 52.5 us -> 48.9 us (0.931)
  local copies, waits for them, and re-layouts: 3.44 us -> 0 us
    unnamed x10 -> x0, local copies, waits for them, and re-layouts: 3.44 us -> none
    pallas_call x1 -> x2, Pallas kernels: 48.2 us -> 48.1 us  [the longest x1 46.7 us: local_step(): pl.pallas_call(kernel, out_shape=(pltpu.VMEM((2, Q, 16, LANES), BF), pltp...]
where the time goes in v4:
time: 48.9 us; the launch traced here: 48.7 us
  Pallas kernels  48.1 us (98%)
  between operations  0.64 us (1%)
    pallas_call x1, Pallas kernels, local_step(): pl.pallas_call(kernel, out_shape=(pltpu.VMEM((2, Q, 16, LANES), BF), pltp...  46.7 us
    pallas_call x1, Pallas kernels, local_step(): pl.pallas_call(finish_kernel, out_shape=(jax.ShapeDtypeStruct((2, Q, 16,...  1.34 us

profile of v4, /device:TPU:1, one launch (start us, length us, event | category | flops | bytes accessed | tf_op | source)
XLA Modules:
  0.0 48.7 jit_solution(4132287759842584611)
XLA Ops:
  0.6 46.7 %shard_map.93 = (bf16[2,19,16,256]{3,2,1,0:T(8,128)(2,1)S(1)}, f32[32,2,128]{2,1,0:T(2,128)S(1)}) custom-call(f32[2,19,16,256]{3,2,1,0:T(8,128)} %pops_hbm.1, bf16[2,19,16,256]{3,2,1,0:T(8,128)(2,1)} %cot_hbm.1, s32[2,16,256]{2,1,0:T(8,128)} %refs_0_.1, bf16[19,128]{1,0:T(8,128)(2,1)} %bitcast.4, f32[1,128]{1,0:T(1,128)} %bitcast.5, bf16[19,128]{1,0:T(8,128)(2,1)} %refs_3_.1), custom_call_target="tpu_custom_call" | custom-call | tf_op jit(solution)/shard_map/pallas_call | solution.py:565
  47.4 1.3 %shard_map.94 = (bf16[2,19,16,256]{3,2,1,0:T(8,128)(2,1)}, f32[19,128]{1,0:T(8,128)}, f32[1,128]{1,0:T(1,128)}, f32[19,128]{1,0:T(8,128)}) custom-call(bf16[2,19,16,256]{3,2,1,0:T(8,128)(2,1)S(1)} %get-tuple-element.10.d0, f32[32,2,128]{2,1,0:T(2,128)S(1)} %get-tuple-element.11.ag), custom_call_target="tpu_custom_call" | custom-call | tf_op jit(solution)/shard_map/pallas_call | solution.py:608

commit v5 on v4

--- a/solution.py
+++ b/solution.py
@@ -49,6 +49,7 @@
 DEV_Z = 16
 PLANE = 32
 CHUNK = 256
+HALF = 128
 BF = jnp.bfloat16
 F32 = jnp.float32
 NT = (((1,), (1,)), ((), ()))
@@ -60,23 +61,23 @@
         (self.own, self.sxp, self.sxm, self.syp, self.sym, self.rxl, self.rxr,
          self.ryl, self.ryu, self.rc, self.send, self.recv) = refs
 
-    def put(self, j, p, s, val):
+    def put(self, j, p, s, val, lanes=slice(None)):
         cx, cy, cz = VELOCITY[j]
         if cz:
             val = pltpu.roll(val, cz % LANES, 1)
         rows = pl.ds(8 * s, 8)
         if cx == 1 and p == 1:
-            self.sxp[X_PLUS.index(j), rows, :] = val
+            self.sxp[X_PLUS.index(j), rows, lanes] = val
         elif cx == -1 and p == 0:
-            self.sxm[X_MINUS.index(j), rows, :] = val
+            self.sxm[X_MINUS.index(j), rows, lanes] = val
         else:
-            self.own[p, j, rows, :] = val
+            self.own[p, j, rows, lanes] = val
         if cy == 1 and s == 1 and (j, p) in Y_PLUS:
             k = Y_PLUS.index((j, p))
-            self.syp[k : k + 1, :] = val[7:8, :]
+            self.syp[k : k + 1, lanes] = val[7:8, :]
         if cy == -1 and s == 0 and (j, p) in Y_MINUS:
             k = Y_MINUS.index((j, p))
-            self.sym[k : k + 1, :] = val[0:1, :]
+            self.sym[k : k + 1, lanes] = val[0:1, :]
 
     def send_half(self, s, near):
         rows = pl.ds(8 * s, 8)
@@ -99,7 +100,7 @@
             c.start()
         return made
 
-    def get(self, j, p, s):
+    def get(self, j, p, s, lanes=slice(None)):
         cx, cy, cz = VELOCITY[j]
         q = p - cx
         if q == -1:
@@ -109,25 +110,26 @@
         else:
             src = self.own.at[q, j]
         if cy == 0:
-            return src[8 * s : 8 * s + 8, :]
-        row = lax.broadcasted_iota(jnp.int32, (8, LANES), 0)
+            return src[8 * s : 8 * s + 8, lanes]
         if cy == 1:
             if s == 1:
-                return src[7:15, :]
+                return src[7:15, lanes]
             if q in (0, 1):
                 k = Y_PLUS.index((j, q))
-                halo = self.ryl[k : k + 1, :]
+                halo = self.ryl[k : k + 1, lanes]
             else:
-                halo = self.rc[CORNERS.index(j), 7:8, :]
-            return jnp.where(row == 0, halo, pltpu.roll(src[0:8, :], 1, 0))
+                halo = self.rc[CORNERS.index(j), 7:8, lanes]
+            main = pltpu.roll(src[0:8, lanes], 1, 0)
+            return jnp.where(iota(main.shape, 0) == 0, halo, main)
         if s == 0:
-            return src[1:9, :]
+            return src[1:9, lanes]
         if q in (0, 1):
             k = Y_MINUS.index((j, q))
-            halo = self.ryu[k : k + 1, :]
+            halo = self.ryu[k : k + 1, lanes]
         else:
-            halo = self.rc[CORNERS.index(j), 0:1, :]
-        return jnp.where(row == 7, halo, pltpu.roll(src[8:16, :], 7, 0))
+            halo = self.rc[CORNERS.index(j), 0:1, lanes]
+        main = pltpu.roll(src[8:16, lanes], 7, 0)
+        return jnp.where(iota(main.shape, 0) == 7, halo, main)
 
 
 EX_SCRATCH = [
@@ -244,31 +246,60 @@
 
 class Reduction:
     def __init__(self, refs, ag, gx, gy):
-        (self.pay, self.rs_in, self.z_own, self.z_in, self.ag_own, self.send, self.recv) = refs
+        (self.pay, self.rs_in, self.z_own, self.z_in, self.ag_own, self.send, self.recv,
+         self.known) = refs
         self.ag = ag
         self.z = lax.rem(gx // 2, DEV_Z)
         core, y = lax.rem(gx, 2), gx // (2 * DEV_Z)
+        self.gx, self.gy, self.core, self.y = gx, gy, core, y
         self.me = y * 8 + gy * 2 + core
         cs = [core, 1 - core]
         xs = [gy] + [lax.rem(gy + k, 4) for k in range(1, 4)]
         ys = [y] + [lax.rem(y + k, 4) for k in range(1, 4)]
-        self.plane = []
+        self.plane, far = [], []
         for dy in range(4):
             base, mbase = ys[dy] * (2 * DEV_Z) + self.z * 2, ys[dy] * 8
             for dc in range(2):
                 for dx in range(4):
                     if dx or dy or dc:
                         dev = (base + cs[dc], xs[dx])
+                        far.append((-min(dx, 4 - dx) - min(dy, 4 - dy), len(far)))
                         self.plane.append((mbase + (xs[dx] * 2 + cs[dc]), dev))
+        self.plane = [self.plane[k] for _, k in sorted(far)]
         line = gx - 2 * self.z
         self.line = []
-        for k in range(1, DEV_Z):
+        for k in sorted(range(1, DEV_Z), key=lambda k: -min(k, DEV_Z - k)):
             self.line.append((line + 2 * lax.rem(self.z + k, DEV_Z), gy))
 
     def greet(self, barrier):
-        for dev in [d for _, d in self.plane] + self.line:
+        for dev in self.axis("z", 1) + self.axis("y", 1):
             pl.semaphore_signal(barrier, inc=1, device_id=dev, device_id_type=MESH)
-        return PLANE + DEV_Z - 2
+        return 4
+
+    def axis(self, name, k):
+        if name == "z":
+            base = self.gx - 2 * self.z
+            return [
+                (base + 2 * lax.rem(self.z + d, DEV_Z), self.gy) for d in (k, DEV_Z - k)
+            ]
+        if name == "y":
+            base = self.gx - self.y * (2 * DEV_Z)
+            return [
+                (base + (2 * DEV_Z) * lax.rem(self.y + d, 4), self.gy) for d in (k, 4 - k)
+            ]
+        if name == "x":
+            return [(self.gx, lax.rem(self.gy + d, 4)) for d in (k, 4 - k)]
+        return [(self.gx - self.core + (1 - self.core), self.gy)]
+
+    def tell(self, step):
+        peers = self.axis("y", 1) + self.axis("x", 1) + self.axis("core", 1)
+        if step < 3:
+            peers = self.axis("z", 2**step) + peers
+        for dev in peers:
+            pl.semaphore_signal(self.known.at[step], inc=1, device_id=dev, device_id_type=MESH)
+
+    def hear(self, step):
+        pl.semaphore_wait(self.known.at[step], 7 if step < 3 else 5)
 
     def remote(self, src, dst, phase, dev):
         return pltpu.make_async_remote_copy(
@@ -316,6 +347,7 @@
     pltpu.VMEM((2, UNITS), F32),
     pltpu.SemaphoreType.DMA((3,)),
     pltpu.SemaphoreType.DMA((3,)),
+    pltpu.SemaphoreType.REGULAR((4,)),
 ]
 N_RED = len(RED_SCRATCH)
 
@@ -323,8 +355,8 @@
 def kernel(pops_hbm, cot_hbm, *refs):
     small_hbm, (out, ag), scratch = refs[:4], refs[4:6], refs[6:]
     gx, gy = lax.axis_index("gx"), lax.axis_index("gy")
-    (w1, w1t, w2, w2t, feat0, feat1, qa, qb, hid0, hid1, ra, rb, t0, t1, gh, field, grad,
-     mom0, post, fold_out, pops, cot, flags, w_in_t, b_in, w_out, in_sem) = scratch[N_RED + 3 * N_EX :]
+    (w1, w1t, w2, w2t, feat0, feat1, qa, qb, hid0, hid1, ra, rb, t0, gh, grad,
+     mom0, mom1, post, tot_ref, pops, cot, flags, w_in_t, b_in, w_out, in_sem) = scratch[N_RED + 3 * N_EX :]
     get_cot = pltpu.make_async_copy(cot_hbm, cot, in_sem.at[0])
     get_pops = pltpu.make_async_copy(pops_hbm, pops, in_sem.at[1])
     gets = [
@@ -365,46 +397,60 @@
             wide = cot[p, i].astype(F32)
             for s in range(2):
                 ex_c.put(OPPOSITE[i], p, s, wide[8 * s : 8 * s + 8, :])
-    one = jnp.ones((8, LANES), F32)
-    nil = jnp.zeros((8, LANES), F32)
+    one = jnp.ones((8, HALF), F32)
+    nil = jnp.zeros((8, HALF), F32)
     get_pops.wait()
     gets[0].wait()
 
-    def lanes_of(p, s):
-        return pl.ds((2 * p + s) * LANES, LANES)
+    def lanes_of(p, s, h=None):
+        first = (2 * p + s) * LANES
+        return pl.ds(first, LANES) if h is None else pl.ds(first + h * HALF, HALF)
 
     def rows_of(s):
         return pl.ds(8 * s, 8)
 
-    def melt_of(p, s):
-        return flags[p, rows_of(s), :].astype(F32)
-
-    def front(f, p, s, feat, hid, act):
-        rho, mom = moments(f)
-        eq = equilibrium(rho, mom)
+    halves = [pl.ds(h * HALF, HALF) for h in range(LANES // HALF)]
+
+    def melt_of(p, s, h):
+        return flags[p, rows_of(s), h].astype(F32)
+
+    def front(read, p, s, feat, mom_ref, rest):
+        for k, h in enumerate(halves):
+            f = [read(i, h) for i in range(Q)]
+            rho, mom = moments(f)
+            for d in range(3):
+                mom_ref[2 * p + s, d, :, h] = mom[d]
+            eq = equilibrium(rho, mom)
+            store_features(
+                feat, lanes_of(p, s, k), [f[i] * INV_W[i] - eq[i] for i in range(Q)] + [one]
+            )
+            if rest is not None:
+                rest(h, f, rho, eq)
+
+    def step_a(p, s):
+        g = 2 * p + s
+
+        def rest(h, f, rho, eq):
+            melt = melt_of(p, s, h) > 0.5
+            excess = rho - 1.0
+            for i in range(Q):
+                val = -0.25 * f[i] + (1.25 * W[i]) * eq[i]
+                cz = VELOCITY[i][2]
+                if cz:
+                    val = val + (0.15 * W[i] * cz) * excess
+                post[g, i, :, h] = jnp.where(melt, val, f[OPPOSITE[i]])
+
+        front(lambda i, h: pops[p, i, rows_of(s), h], p, s, feat0, mom0, rest)
         lanes = lanes_of(p, s)
-        store_features(feat, lanes, [f[i] * INV_W[i] - eq[i] for i in range(Q)] + [one])
         for c in range(0, HID, CHUNK):
             block = pl.ds(c, CHUNK)
-            t = jnp.tanh(dot(w1[block, :], feat[:, lanes]))
-            act[block, lanes] = t
-            hid[block, lanes] = t.astype(BF)
-        return rho, mom, eq
-
-    def step_a(p, s):
-        f = [pops[p, i, rows_of(s), :] for i in range(Q)]
-        rho, mom, eq = front(f, p, s, feat0, hid0, t0)
-        for d in range(3):
-            mom0[2 * p + s, d] = mom[d]
-        learned = dot(w2[...], hid0[:, lanes_of(p, s)])
-        melt = melt_of(p, s) > 0.5
-        excess = rho - 1.0
+            t = jnp.tanh(dot(w1[block, :], feat0[:, lanes]))
+            t0[block, lanes] = t
+            hid0[block, lanes] = t.astype(BF)
+        learned = dot(w2[...], hid0[:, lanes])
+        melt = melt_of(p, s, slice(None)) > 0.5
         for i in range(Q):
-            val = -0.25 * f[i] + (1.25 * W[i]) * eq[i] + learned[8 * i : 8 * i + 8, :]
-            cz = VELOCITY[i][2]
-            if cz:
-                val = val + (0.15 * W[i] * cz) * excess
-            ex_p.put(i, p, s, jnp.where(melt, val, f[OPPOSITE[i]]))
+            ex_p.put(i, p, s, post[g, i] + jnp.where(melt, learned[8 * i : 8 * i + 8, :], 0.0))
 
     copies_c, copies_p, copies_d = [], [], []
     for p in range(2):
@@ -416,127 +462,151 @@
     for p in range(2):
         step_a(p, 0)
     copies_p += ex_p.send_half(0, near)
+    reduction.tell(0)
 
     tall(w_out[...], w2t)
     flat(w_in_t[...], w1t)
+    tot_ref[...] = jnp.zeros((2, ROWS, UNITS), F32)
     for c in copies_c:
         c.wait()
 
-    def hidden_grad(p, s, q):
-        melt = melt_of(p, s)
-        m = [grad[2 * p + s, i] * melt for i in range(Q)]
-        store_features(q, lanes_of(p, s), m + [nil])
+    def take(ex, p, s, q):
+        for k, h in enumerate(halves):
+            melt = melt_of(p, s, h)
+            m = []
+            for i in range(Q):
+                val = ex.get(OPPOSITE[i], p, s, h)
+                grad[2 * p + s, i, :, h] = val
+                m.append(val * melt)
+            store_features(q, lanes_of(p, s, k), m + [nil])
 
     for p in range(2):
         for s in range(2):
-            for i in range(Q):
-                grad[2 * p + s, i] = ex_c.get(OPPOSITE[i], p, s)
-            hidden_grad(p, s, qb)
+            take(ex_c, p, s, qb)
+            lanes = lanes_of(p, s)
             for c in range(0, HID, CHUNK):
                 block = pl.ds(c, CHUNK)
-                gh[block, lanes_of(p, s)] = dot(w2t[block, :], qb[:, lanes_of(p, s)])
-
+                gh[block, lanes] = dot(w2t[block, :], qb[:, lanes])
+
+    @pl.loop(0, HID // 32)
+    def _(k):
+        block = pl.ds(pl.multiple_of(32 * k, 32), 32)
+        t = t0[block, :]
+        t0[block, :] = 1.0 - t * t
+
+    reduction.hear(0)
+    reduction.tell(1)
     for c in copies_p:
         c.wait()
 
-    def back(p, s, mom, r, put):
+    def back(p, s, mom_ref, r, put):
         g = 2 * p + s
-        melt = melt_of(p, s)
         prod = dot(w1t[...], r[:, lanes_of(p, s)])
-        m, wd = [], []
-        for i in range(Q):
-            m.append(grad[g, i] * melt)
-            wd.append((1.25 * W[i]) * m[i] - prod[8 * i : 8 * i + 8, :])
-        total = wd[0]
-        lift = None
-        dj = [None, None, None]
-        for a, b in PAIRS:
-            both = wd[a] + wd[b]
-            total = total + both
-            cz = VELOCITY[a][2]
-            if cz:
-                term = (0.15 * W[a] * cz) * (m[a] - m[b])
-                lift = term if lift is None else lift + term
-            slope = 3.0 * (wd[a] - wd[b]) + 9.0 * along(a, mom) * both
-            for d in range(3):
-                c = VELOCITY[a][d]
-                if c == 0:
-                    continue
-                if dj[d] is None:
-                    dj[d] = slope if c == 1 else -slope
-                else:
-                    dj[d] = dj[d] + slope if c == 1 else dj[d] - slope
-        drho = total + lift
-        dj = [dj[d] - 3.0 * mom[d] * total for d in range(3)]
-        for i in range(Q):
-            o = OPPOSITE[i]
-            val = (-0.25) * m[i] + INV_W[i] * prod[8 * i : 8 * i + 8, :] + drho
-            if i:
-                val = val + along(i, dj)
-            put(i, val + (grad[g, o] - m[o]))
+        for k, h in enumerate(halves):
+            melt = melt_of(p, s, h)
+            mom = [mom_ref[g, d, :, h] for d in range(3)]
+            pr = [prod[8 * i : 8 * i + 8, HALF * k : HALF * (k + 1)] for i in range(Q)]
+            m = [grad[g, i, :, h] * melt for i in range(Q)]
+            wd = [(1.25 * W[i]) * m[i] - pr[i] for i in range(Q)]
+            total = wd[0]
+            lift = None
+            dj = [None, None, None]
+            for a, b in PAIRS:
+                both = wd[a] + wd[b]
+                total = total + both
+                cz = VELOCITY[a][2]
+                if cz:
+                    term = (0.15 * W[a] * cz) * (m[a] - m[b])
+                    lift = term if lift is None else lift + term
+                slope = 3.0 * (wd[a] - wd[b]) + 9.0 * along(a, mom) * both
+                for d in range(3):
+                    c = VELOCITY[a][d]
+                    if c == 0:
+                        continue
+                    if dj[d] is None:
+                        dj[d] = slope if c == 1 else -slope
+                    else:
+                        dj[d] = dj[d] + slope if c == 1 else dj[d] - slope
+            drho = total + lift
+            dj = [dj[d] - 3.0 * mom[d] * total for d in range(3)]
+            put(h, 0, (-0.25) * m[0] + INV_W[0] * pr[0] + drho + (grad[g, 0, :, h] - m[0]))
+            for a, b in PAIRS:
+                turn = along(a, dj)
+                for i, o, base in ((a, b, drho + turn), (b, a, drho - turn)):
+                    val = (-0.25) * m[i] + INV_W[i] * pr[i] + base
+                    put(h, i, val + (grad[g, o, :, h] - m[o]))
 
     def step_b(p, s):
-        f = [ex_p.get(i, p, s) for i in range(Q)]
-        _, mom, _ = front(f, p, s, feat1, hid1, t1)
+        g = 2 * p + s
+        front(lambda i, h: ex_p.get(i, p, s, h), p, s, feat1, mom1, None)
         lanes = lanes_of(p, s)
         for c in range(0, HID, CHUNK):
             block = pl.ds(c, CHUNK)
-            t = t1[block, lanes]
+            t = jnp.tanh(dot(w1[block, :], feat1[:, lanes]))
+            hid1[block, lanes] = t.astype(BF)
             rb[block, lanes] = (gh[block, lanes] * (1.0 - t * t)).astype(BF)
-        back(p, s, mom, rb, lambda i, val: ex_d.put(OPPOSITE[i], p, s, val))
+
+        def put(h, i, val):
+            if VELOCITY[i][2]:
+                post[g, i, :, h] = val
+            else:
+                ex_d.put(OPPOSITE[i], p, s, val, h)
+
+        back(p, s, mom1, rb, put)
+        for i in range(Q):
+            if VELOCITY[i][2]:
+                ex_d.put(OPPOSITE[i], p, s, post[g, i])
 
     for s in (1, 0):
         for p in range(2):
             step_b(p, s)
         copies_d += ex_d.send_half(s, near)
 
-    def weight_sums(feat, r, q, hid):
-        sub = iota((ROWS, UNITS), 0) % 8
-        sums = []
-        for left, right in ((feat, r), (q, hid)):
-            tot = None
-            for c in range(0, HID, 256):
-                acc = dot(left[:ROWS, :], right[pl.ds(c, 256), :], NT)
-                for k in range(2):
-                    hit = jnp.where(sub == c // UNITS + k, acc[:, UNITS * k : UNITS * (k + 1)], 0.0)
-                    tot = hit if tot is None else tot + hit
-            sums.append(jnp.sum(tot.reshape(20, 8, UNITS), axis=1))
-        return sums
-
-    for k, val in enumerate(weight_sums(feat1, rb, qb, hid1)):
-        fold_out[0, k] = val
-    for c in range(0, HID, CHUNK):
-        block = pl.ds(c, CHUNK)
-        t = t0[block, :]
-        t0[block, :] = 1.0 - t * t
-
+    sub = iota((ROWS, UNITS), 0) % 8
+
+    reduction.hear(1)
+    reduction.tell(2)
+
+    @pl.loop(0, HID // 256)
+    def _(c):
+        block = pl.ds(pl.multiple_of(256 * c, 256), 256)
+        for k, (left, right) in enumerate(((qb, hid1), (feat1, rb))):
+            acc = dot(left[:ROWS, :], right[block, :], NT)
+            tot_ref[k] += jnp.where(sub == 2 * c, acc[:, :UNITS], 0.0) + jnp.where(
+                sub == 2 * c + 1, acc[:, UNITS:], 0.0
+            )
+
+    reduction.hear(2)
+    reduction.tell(3)
     for c in copies_d:
         c.wait()
     for p in range(2):
         for s in range(2):
-            for i in range(Q):
-                grad[2 * p + s, i] = ex_d.get(OPPOSITE[i], p, s)
-            hidden_grad(p, s, qa)
+            take(ex_d, p, s, qa)
             lanes = lanes_of(p, s)
             for c in range(0, HID, CHUNK):
                 block = pl.ds(c, CHUNK)
                 ra[block, lanes] = (dot(w2t[block, :], qa[:, lanes]) * t0[block, lanes]).astype(BF)
 
-    for k, val in enumerate(weight_sums(feat0, ra, qa, hid0)):
-        tot = val + fold_out[0, k]
+    for k, (left, right) in enumerate(((qa, hid0), (feat0, ra))):
+        tot = tot_ref[k]
+        for c in range(HID // 256):
+            acc = dot(left[:ROWS, :], right[pl.ds(256 * c, 256), :], NT)
+            for y in range(2):
+                tot = tot + jnp.where(sub == 2 * c + y, acc[:, UNITS * y : UNITS * (y + 1)], 0.0)
+        tot = jnp.sum(tot.reshape(20, 8, UNITS), axis=1)
         for j in range(10):
-            reduction.pay[10 * k + j] = tot[2 * j : 2 * j + 2, :]
+            reduction.pay[10 * (1 - k) + j] = tot[2 * j : 2 * j + 2, :]
+    reduction.hear(3)
     reduction.scatter()
-
-    def keep(p, s):
-        def put(i, val):
-            post[2 * p + s, i] = val
-
-        return put
 
     for p in range(2):
         for s in range(2):
-            back(p, s, [mom0[2 * p + s, d] for d in range(3)], ra, keep(p, s))
+
+            def put(h, i, val):
+                post[2 * p + s, i, :, h] = val
+
+            back(p, s, mom0, ra, put)
         for i in range(Q):
             out[p, i] = jnp.concatenate([post[2 * p, i], post[2 * p + 1, i]], axis=0).astype(BF)
     reduction.finish()
@@ -587,12 +657,11 @@
             pltpu.VMEM((HID, cells), BF),
             pltpu.VMEM((HID, cells), F32),
             pltpu.VMEM((HID, cells), F32),
-            pltpu.VMEM((HID, cells), F32),
-            pltpu.VMEM((GROUPS, Q, 8, LANES), F32),
             pltpu.VMEM((GROUPS, Q, 8, LANES), F32),
             pltpu.VMEM((GROUPS, 3, 8, LANES), F32),
+            pltpu.VMEM((GROUPS, 3, 8, LANES), F32),
             pltpu.VMEM((GROUPS, Q, 8, LANES), F32),
-            pltpu.VMEM((2, 2, 20, UNITS), F32),
+            pltpu.VMEM((2, ROWS, UNITS), F32),
             pltpu.VMEM((2, Q, 16, LANES), F32),
             pltpu.VMEM((2, Q, 16, LANES), BF),
             pltpu.VMEM((2, 16, LANES), jnp.int32),

time: 48.9 us -> 46.6 us (0.953)
  Pallas kernels: 48.1 us -> 45.8 us
    pallas_call x1, Pallas kernels: 46.7 us -> 44.5 us  [local_step(): pl.pallas_call(kernel, out_shape=(pltpu.VMEM((2, Q, 16, LANES), BF), pltp...]
where the time goes in v5:
time: 46.6 us; the launch traced here: 46.5 us
  Pallas kernels  45.8 us (98%)
  between operations  0.64 us (1%)
    pallas_call x1, Pallas kernels, local_step(): pl.pallas_call(kernel, out_shape=(pltpu.VMEM((2, Q, 16, LANES), BF), pltp...  44.5 us
    pallas_call x1, Pallas kernels, local_step(): pl.pallas_call(finish_kernel, out_shape=(jax.ShapeDtypeStruct((2, Q, 16,...  1.34 us

profile of v5, /device:TPU:1, one launch (start us, length us, event | category | flops | bytes accessed | tf_op | source)
XLA Modules:
  0.0 46.5 jit_solution(12552119432052989048)
XLA Ops:
  0.6 44.5 %shard_map.93 = (bf16[2,19,16,256]{3,2,1,0:T(8,128)(2,1)S(1)}, f32[32,2,128]{2,1,0:T(2,128)S(1)}) custom-call(f32[2,19,16,256]{3,2,1,0:T(8,128)} %pops_hbm.1, bf16[2,19,16,256]{3,2,1,0:T(8,128)(2,1)} %cot_hbm.1, s32[2,16,256]{2,1,0:T(8,128)} %refs_0_.1, bf16[19,128]{1,0:T(8,128)(2,1)} %bitcast.4, f32[1,128]{1,0:T(1,128)} %bitcast.5, bf16[19,128]{1,0:T(8,128)(2,1)} %refs_3_.1), custom_call_target="tpu_custom_call" | custom-call | tf_op jit(solution)/shard_map/pallas_call | solution.py:635
  45.1 1.3 %shard_map.94 = (bf16[2,19,16,256]{3,2,1,0:T(8,128)(2,1)}, f32[19,128]{1,0:T(8,128)}, f32[1,128]{1,0:T(1,128)}, f32[19,128]{1,0:T(8,128)}) custom-call(bf16[2,19,16,256]{3,2,1,0:T(8,128)(2,1)S(1)} %get-tuple-element.10.d0, f32[32,2,128]{2,1,0:T(2,128)S(1)} %get-tuple-element.11.ag), custom_call_target="tpu_custom_call" | custom-call | tf_op jit(solution)/shard_map/pallas_call | solution.py:677

commit v6 on v5

--- a/solution.py
+++ b/solution.py
@@ -386,21 +386,13 @@
     for c in gets[1:]:
         c.wait()
     tall(w_in_t[...], w1, bias_columns(b_in[...]))
-    flat(w_out[...], w2)
     zero = jnp.zeros((DEPTH - ROWS, GROUPS * LANES), BF)
     for ref in (feat0, feat1, qa, qb):
         ref[ROWS:, :] = zero
     reduction.pay[...] = jnp.zeros((PLANE, 2, UNITS), F32)
-    get_cot.wait()
-    for p in range(2):
-        for i in range(Q):
-            wide = cot[p, i].astype(F32)
-            for s in range(2):
-                ex_c.put(OPPOSITE[i], p, s, wide[8 * s : 8 * s + 8, :])
-    one = jnp.ones((8, HALF), F32)
-    nil = jnp.zeros((8, HALF), F32)
     get_pops.wait()
     gets[0].wait()
+    get_cot.wait()
 
     def lanes_of(p, s, h=None):
         first = (2 * p + s) * LANES
@@ -427,7 +419,7 @@
             if rest is not None:
                 rest(h, f, rho, eq)
 
-    def step_a(p, s):
+    def start_a(p, s):
         g = 2 * p + s
 
         def rest(h, f, rho, eq):
@@ -441,26 +433,42 @@
                 post[g, i, :, h] = jnp.where(melt, val, f[OPPOSITE[i]])
 
         front(lambda i, h: pops[p, i, rows_of(s), h], p, s, feat0, mom0, rest)
+
+    def net_a(p, s):
         lanes = lanes_of(p, s)
         for c in range(0, HID, CHUNK):
             block = pl.ds(c, CHUNK)
             t = jnp.tanh(dot(w1[block, :], feat0[:, lanes]))
             t0[block, lanes] = t
             hid0[block, lanes] = t.astype(BF)
-        learned = dot(w2[...], hid0[:, lanes])
+
+    def end_a(p, s):
+        g = 2 * p + s
+        learned = dot(w2[...], hid0[:, lanes_of(p, s)])
         melt = melt_of(p, s, slice(None)) > 0.5
         for i in range(Q):
             ex_p.put(i, p, s, post[g, i] + jnp.where(melt, learned[8 * i : 8 * i + 8, :], 0.0))
 
+    def pair_a(s):
+        for stage in (start_a, net_a, end_a):
+            for p in range(2):
+                stage(p, s)
+
     copies_c, copies_p, copies_d = [], [], []
+    flat(w_out[...], w2)
     for p in range(2):
-        step_a(p, 1)
+        for i in range(Q):
+            wide = cot[p, i].astype(F32)
+            for s in range(2):
+                ex_c.put(OPPOSITE[i], p, s, wide[8 * s : 8 * s + 8, :])
+    one = jnp.ones((8, HALF), F32)
+    nil = jnp.zeros((8, HALF), F32)
+    pair_a(1)
     pl.semaphore_wait(barrier, greeted)
     copies_c += ex_c.send_half(1, near)
     copies_c += ex_c.send_half(0, near)
     copies_p += ex_p.send_half(1, near)
-    for p in range(2):
-        step_a(p, 0)
+    pair_a(0)
     copies_p += ex_p.send_half(0, near)
     reduction.tell(0)
 
@@ -536,9 +544,10 @@
                     val = (-0.25) * m[i] + INV_W[i] * pr[i] + base
                     put(h, i, val + (grad[g, o, :, h] - m[o]))
 
-    def step_b(p, s):
-        g = 2 * p + s
+    def start_b(p, s):
         front(lambda i, h: ex_p.get(i, p, s, h), p, s, feat1, mom1, None)
+
+    def net_b(p, s):
         lanes = lanes_of(p, s)
         for c in range(0, HID, CHUNK):
             block = pl.ds(c, CHUNK)
@@ -546,6 +555,9 @@
             hid1[block, lanes] = t.astype(BF)
             rb[block, lanes] = (gh[block, lanes] * (1.0 - t * t)).astype(BF)
 
+    def end_b(p, s):
+        g = 2 * p + s
+
         def put(h, i, val):
             if VELOCITY[i][2]:
                 post[g, i, :, h] = val
@@ -558,8 +570,9 @@
                 ex_d.put(OPPOSITE[i], p, s, post[g, i])
 
     for s in (1, 0):
-        for p in range(2):
-            step_b(p, s)
+        for stage in (start_b, net_b, end_b):
+            for p in range(2):
+                stage(p, s)
         copies_d += ex_d.send_half(s, near)
 
     sub = iota((ROWS, UNITS), 0) % 8
@@ -612,8 +625,8 @@
     reduction.finish()
 
 
-def finish_kernel(d0, ag, d0_ref, gin_ref, gb_ref, gout_ref, sem):
-    write = pltpu.make_async_copy(d0, d0_ref, sem)
+def finish_kernel(d0, ag, d0_ref, gin_ref, gb_ref, gout_ref, gin, gb, gout, sem):
+    write = pltpu.make_async_copy(d0, d0_ref, sem.at[0])
     write.start()
 
     def normalized(rows):
@@ -622,9 +635,17 @@
         return total / jnp.sqrt(scale)
 
     row = [ag[k // 2, k % 2 : k % 2 + 1, :] for k in range(2 * 20)]
-    gin_ref[...] = normalized(row[:Q])
-    gb_ref[...] = normalized(row[Q : Q + 1])
-    gout_ref[...] = normalized(row[Q + 1 : 2 * Q + 1])
+    gin[...] = normalized(row[:Q])
+    gb[...] = normalized(row[Q : Q + 1])
+    gout[...] = normalized(row[Q + 1 : 2 * Q + 1])
+    small = [
+        pltpu.make_async_copy(src, dst, sem.at[1 + k])
+        for k, (src, dst) in enumerate(((gin, gin_ref), (gb, gb_ref), (gout, gout_ref)))
+    ]
+    for c in small:
+        c.start()
+    for c in small:
+        c.wait()
     write.wait()
 
 
@@ -683,8 +704,13 @@
             jax.ShapeDtypeStruct((Q, UNITS), F32),
         ),
         in_specs=[vmem] * 2,
-        out_specs=(hbm, vmem, vmem, vmem),
-        scratch_shapes=[pltpu.SemaphoreType.DMA],
+        out_specs=(hbm,) * 4,
+        scratch_shapes=[
+            pltpu.VMEM((Q, UNITS), F32),
+            pltpu.VMEM((1, UNITS), F32),
+            pltpu.VMEM((Q, UNITS), F32),
+            pltpu.SemaphoreType.DMA((4,)),
+        ],
         compiler_params=pltpu.CompilerParams(vmem_limit_bytes=1024 * 1024),
     )(d0, ag)
 

time: 46.6 us -> 45.8 us (0.983)
  Pallas kernels: 45.8 us -> 45 us
where the time goes in v6:
time: 45.8 us; the launch traced here: 45.6 us
  Pallas kernels  45 us (98%)
  between operations  0.64 us (1%)
    pallas_call x1, Pallas kernels, local_step(): pl.pallas_call(kernel, out_shape=(pltpu.VMEM((2, Q, 16, LANES), BF), pltp...  44.1 us

profile of v6, /device:TPU:1, one launch (start us, length us, event | category | flops | bytes accessed | tf_op | source)
XLA Modules:
  0.0 45.6 jit_solution(1658992586274484567)
XLA Ops:
  0.6 44.1 %shard_map.93 = (bf16[2,19,16,256]{3,2,1,0:T(8,128)(2,1)S(1)}, f32[32,2,128]{2,1,0:T(2,128)S(1)}) custom-call(f32[2,19,16,256]{3,2,1,0:T(8,128)} %pops_hbm.1, bf16[2,19,16,256]{3,2,1,0:T(8,128)(2,1)} %cot_hbm.1, s32[2,16,256]{2,1,0:T(8,128)} %refs_0_.1, bf16[19,128]{1,0:T(8,128)(2,1)} %bitcast.4, f32[1,128]{1,0:T(1,128)} %bitcast.5, bf16[19,128]{1,0:T(8,128)(2,1)} %refs_3_.1), custom_call_target="tpu_custom_call" | custom-call | tf_op jit(solution)/shard_map/pallas_call | solution.py:656
  44.7 0.9 %shard_map.94 = (bf16[2,19,16,256]{3,2,1,0:T(8,128)(2,1)}, f32[19,128]{1,0:T(8,128)}, f32[1,128]{1,0:T(1,128)}, f32[19,128]{1,0:T(8,128)}) custom-call(bf16[2,19,16,256]{3,2,1,0:T(8,128)(2,1)S(1)} %get-tuple-element.10.d0, f32[32,2,128]{2,1,0:T(2,128)S(1)} %get-tuple-element.11.ag), custom_call_target="tpu_custom_call" | custom-call | tf_op jit(solution)/shard_map/pallas_call | solution.py:698

commit v7 on v6

--- a/solution.py
+++ b/solution.py
@@ -463,10 +463,15 @@
                 ex_c.put(OPPOSITE[i], p, s, wide[8 * s : 8 * s + 8, :])
     one = jnp.ones((8, HALF), F32)
     nil = jnp.zeros((8, HALF), F32)
-    pair_a(1)
+    for p in range(2):
+        start_a(p, 1)
+    for p in range(2):
+        net_a(p, 1)
     pl.semaphore_wait(barrier, greeted)
     copies_c += ex_c.send_half(1, near)
     copies_c += ex_c.send_half(0, near)
+    for p in range(2):
+        end_a(p, 1)
     copies_p += ex_p.send_half(1, near)
     pair_a(0)
     copies_p += ex_p.send_half(0, near)
@@ -591,11 +596,37 @@
 
     reduction.hear(2)
     reduction.tell(3)
-    for c in copies_d:
-        c.wait()
+    corner_pair = {(0, 0): 8, (1, 0): 8, (1, 1): 6, (0, 1): 10}
+
+    def take_pairs(p, s, late):
+        for k, h in enumerate(halves):
+            melt = melt_of(p, s, h)
+            for i in range(0, Q, 2):
+                if (corner_pair[p, s] == i) != late:
+                    continue
+                both = []
+                for n in (i, i + 1):
+                    if n < Q:
+                        val = ex_d.get(OPPOSITE[n], p, s, h)
+                        grad[2 * p + s, n, :, h] = val
+                        both.append(val * melt)
+                    else:
+                        both.append(nil)
+                two = jnp.concatenate(both, axis=0)
+                qa[8 * i : 8 * i + 16, lanes_of(p, s, k)] = two.astype(BF)
+
+    for half in (copies_d[:5], copies_d[5:]):
+        for c in half[2:]:
+            c.wait()
     for p in range(2):
         for s in range(2):
-            take(ex_d, p, s, qa)
+            take_pairs(p, s, False)
+    for half in (copies_d[:5], copies_d[5:]):
+        for c in half[:2]:
+            c.wait()
+    for p in range(2):
+        for s in range(2):
+            take_pairs(p, s, True)
             lanes = lanes_of(p, s)
             for c in range(0, HID, CHUNK):
                 block = pl.ds(c, CHUNK)

time: 45.8 us -> 45.7 us (level)
  no operation moved by 1% of the time
where the time goes in v7:
time: 45.7 us; the launch traced here: 45.6 us
  Pallas kernels  44.9 us (98%)
  between operations  0.64 us (1%)
    pallas_call x1, Pallas kernels, local_step(): pl.pallas_call(kernel, out_shape=(pltpu.VMEM((2, Q, 16, LANES), BF), pltp...  44 us

profile of v7, /device:TPU:1, one launch (start us, length us, event | category | flops | bytes accessed | tf_op | source)
XLA Modules:
  0.0 45.6 jit_solution(2288031622816538058)
XLA Ops:
  0.6 44.0 %shard_map.93 = (bf16[2,19,16,256]{3,2,1,0:T(8,128)(2,1)S(1)}, f32[32,2,128]{2,1,0:T(2,128)S(1)}) custom-call(f32[2,19,16,256]{3,2,1,0:T(8,128)} %pops_hbm.1, bf16[2,19,16,256]{3,2,1,0:T(8,128)(2,1)} %cot_hbm.1, s32[2,16,256]{2,1,0:T(8,128)} %refs_0_.1, bf16[19,128]{1,0:T(8,128)(2,1)} %bitcast.4, f32[1,128]{1,0:T(1,128)} %bitcast.5, bf16[19,128]{1,0:T(8,128)(2,1)} %refs_3_.1), custom_call_target="tpu_custom_call" | custom-call | tf_op jit(solution)/shard_map/pallas_call | solution.py:687
  44.7 0.9 %shard_map.94 = (bf16[2,19,16,256]{3,2,1,0:T(8,128)(2,1)}, f32[19,128]{1,0:T(8,128)}, f32[1,128]{1,0:T(1,128)}, f32[19,128]{1,0:T(8,128)}) custom-call(bf16[2,19,16,256]{3,2,1,0:T(8,128)(2,1)S(1)} %get-tuple-element.10.d0, f32[32,2,128]{2,1,0:T(2,128)S(1)} %get-tuple-element.11.ag), custom_call_target="tpu_custom_call" | custom-call | tf_op jit(solution)/shard_map/pallas_call | solution.py:729

commit v8 on v6

--- a/solution.py
+++ b/solution.py
@@ -57,7 +57,8 @@
 
 
 class Exchange:
-    def __init__(self, refs):
+    def __init__(self, refs, span):
+        self.span = span
         (self.own, self.sxp, self.sxm, self.syp, self.sym, self.rxl, self.rxr,
          self.ryl, self.ryu, self.rc, self.send, self.recv) = refs
 
@@ -91,14 +92,22 @@
         ]
         made = [
             pltpu.make_async_remote_copy(
-                src_ref=src, dst_ref=dst, send_sem=self.send.at[5 * s + k],
-                recv_sem=self.recv.at[5 * s + k], device_id=dev, device_id_type=MESH,
+                src_ref=src, dst_ref=dst, send_sem=self.send,
+                recv_sem=self.recv, device_id=dev, device_id_type=MESH,
             )
             for k, (src, dst, dev) in enumerate(plan)
         ]
         for c in made:
             c.start()
         return made
+
+    def finish(self, near):
+        every = pltpu.make_async_remote_copy(
+            src_ref=self.span, dst_ref=self.span, send_sem=self.send, recv_sem=self.recv,
+            device_id=near(1, 0), device_id_type=MESH,
+        )
+        every.wait_send()
+        every.wait_recv()
 
     def get(self, j, p, s, lanes=slice(None)):
         cx, cy, cz = VELOCITY[j]
@@ -143,8 +152,8 @@
     pltpu.VMEM((8, LANES), F32),
     pltpu.VMEM((8, LANES), F32),
     pltpu.VMEM((4, 8, LANES), F32),
-    pltpu.SemaphoreType.DMA((10,)),
-    pltpu.SemaphoreType.DMA((10,)),
+    pltpu.SemaphoreType.DMA,
+    pltpu.SemaphoreType.DMA,
 ]
 N_EX = len(EX_SCRATCH)
 
@@ -356,7 +365,7 @@
     small_hbm, (out, ag), scratch = refs[:4], refs[4:6], refs[6:]
     gx, gy = lax.axis_index("gx"), lax.axis_index("gy")
     (w1, w1t, w2, w2t, feat0, feat1, qa, qb, hid0, hid1, ra, rb, t0, gh, grad,
-     mom0, mom1, post, tot_ref, pops, cot, flags, w_in_t, b_in, w_out, in_sem) = scratch[N_RED + 3 * N_EX :]
+     mom0, mom1, post, tot_ref, pops, cot, flags, w_in_t, b_in, w_out, span, in_sem) = scratch[N_RED + 3 * N_EX :]
     get_cot = pltpu.make_async_copy(cot_hbm, cot, in_sem.at[0])
     get_pops = pltpu.make_async_copy(pops_hbm, pops, in_sem.at[1])
     gets = [
@@ -367,7 +376,7 @@
         c.start()
     reduction = Reduction(scratch[:N_RED], ag, gx, gy)
     ex_c, ex_p, ex_d = [
-        Exchange(scratch[N_RED + k * N_EX : N_RED + (k + 1) * N_EX]) for k in range(3)
+        Exchange(scratch[N_RED + k * N_EX : N_RED + (k + 1) * N_EX], span) for k in range(3)
     ]
     step_x = {0: gx, 1: lax.rem(gx + 1, 128), -1: lax.rem(gx + 127, 128)}
     step_y = {0: gy, 1: lax.rem(gy + 1, 4), -1: lax.rem(gy + 3, 4)}
@@ -475,8 +484,7 @@
     tall(w_out[...], w2t)
     flat(w_in_t[...], w1t)
     tot_ref[...] = jnp.zeros((2, ROWS, UNITS), F32)
-    for c in copies_c:
-        c.wait()
+    ex_c.finish(near)
 
     def take(ex, p, s, q):
         for k, h in enumerate(halves):
@@ -504,8 +512,7 @@
 
     reduction.hear(0)
     reduction.tell(1)
-    for c in copies_p:
-        c.wait()
+    ex_p.finish(near)
 
     def back(p, s, mom_ref, r, put):
         g = 2 * p + s
@@ -591,8 +598,7 @@
 
     reduction.hear(2)
     reduction.tell(3)
-    for c in copies_d:
-        c.wait()
+    ex_d.finish(near)
     for p in range(2):
         for s in range(2):
             take(ex_d, p, s, qa)
@@ -689,6 +695,7 @@
             pltpu.VMEM((Q, UNITS), BF),
             pltpu.VMEM((1, UNITS), F32),
             pltpu.VMEM((Q, UNITS), BF),
+            pltpu.VMEM((208, LANES), F32),
             pltpu.SemaphoreType.DMA((6,)),
         ],
         compiler_params=pltpu.CompilerParams(

time: 45.8 us -> 45.2 us (0.987)
  Pallas kernels: 45 us -> 44.4 us
    pallas_call x1, Pallas kernels: 44.1 us -> 43.5 us  [local_step(): pl.pallas_call(kernel, out_shape=(pltpu.VMEM((2, Q, 16, LANES), BF), pltp...]
where the time goes in v8:
time: 45.2 us; the launch traced here: 45.1 us
  Pallas kernels  44.4 us (98%)
  between operations  0.64 us (1%)
    pallas_call x1, Pallas kernels, local_step(): pl.pallas_call(kernel, out_shape=(pltpu.VMEM((2, Q, 16, LANES), BF), pltp...  43.5 us

profile of v8, /device:TPU:1, one launch (start us, length us, event | category | flops | bytes accessed | tf_op | source)
XLA Modules:
  0.0 45.1 jit_solution(15649210630747236051)
XLA Ops:
  0.6 43.5 %shard_map.93 = (bf16[2,19,16,256]{3,2,1,0:T(8,128)(2,1)S(1)}, f32[32,2,128]{2,1,0:T(2,128)S(1)}) custom-call(f32[2,19,16,256]{3,2,1,0:T(8,128)} %pops_hbm.1, bf16[2,19,16,256]{3,2,1,0:T(8,128)(2,1)} %cot_hbm.1, s32[2,16,256]{2,1,0:T(8,128)} %refs_0_.1, bf16[19,128]{1,0:T(8,128)(2,1)} %bitcast.4, f32[1,128]{1,0:T(1,128)} %bitcast.5, bf16[19,128]{1,0:T(8,128)(2,1)} %refs_3_.1), custom_call_target="tpu_custom_call" | custom-call | tf_op jit(solution)/shard_map/pallas_call | solution.py:662
  44.2 0.9 %shard_map.94 = (bf16[2,19,16,256]{3,2,1,0:T(8,128)(2,1)}, f32[19,128]{1,0:T(8,128)}, f32[1,128]{1,0:T(1,128)}, f32[19,128]{1,0:T(8,128)}) custom-call(bf16[2,19,16,256]{3,2,1,0:T(8,128)(2,1)S(1)} %get-tuple-element.10.d0, f32[32,2,128]{2,1,0:T(2,128)S(1)} %get-tuple-element.11.ag), custom_call_target="tpu_custom_call" | custom-call | tf_op jit(solution)/shard_map/pallas_call | solution.py:705
